TPU v7x, 32 devices: a whole 2x2x4 slice. The times are simulated.
32 devices in a mesh: grid: 8 (over z, y), tile: 4 (over x, core).
Axes of the slice: x: 2, y: 2, z: 4, core: 2. Of those that a mesh axis runs over, the one named last changes fastest.
Arguments:
- point_values: bfloat16 [256, 16384], P('grid', 'tile'), may hold values from -1.75 to 1.75
- sig_blocks: int32 [8, 16], P('grid'), may hold values from 0 to 31, as said below
- density: bfloat16 [16384, 16384], P('grid', 'tile'), may hold values from -0.0625 to 0.0625
- coulomb_core: bfloat16 [512, 512], replicated, may hold values from -0.25 to 0.25
- screen_mask: int32 [32, 32], replicated, may hold values 0 or 1
- ao_centers: float32 [3, 16384], replicated, may hold values from -1 to 1
- ao_widths: float32 [16384], replicated, may hold values from 0.25 to 1
- point_coords: float32 [3, 256], P(None, 'grid'), may hold values from -1 to 1
- lmo_coeffs: bfloat16 [16384, 1024], P('tile'), may hold values from -0.0625 to 0.0625
- domain_blocks: int32 [4, 16], replicated, may hold values from 0 to 31, as said below
Outputs:
- half: bfloat16 [1024, 16384], P('tile', 'grid')
Inputs may be any that keep to these rules, and one draw needn't show every extreme that they name: `sig_blocks`: each batch names 16 different AO blocks. `domain_blocks`: each strip's 16 blocks are different, and every AO block lies in the domain of some strip.
All inputs are finite; a program needn't handle non-finite values.
Results may differ from a plain program's by a relative error of at most 0.02.
Values may be sent and summed in bfloat16 or wider, within the bound.
A program may use at most 128 MiB of HBM per device.

v0:
```python
import jax
import jax.numpy as jnp
from jax import lax
from jax.sharding import PartitionSpec as P

highest = lax.Precision.HIGHEST


def kernel_weights(ao_centers, ao_widths, point_coords):
    offsets = ao_centers[:, None, :] - point_coords[:, :, None]
    return 1.0 / jnp.sqrt(jnp.sum(offsets * offsets, axis=0) + ao_widths[None, :])


def spread_mask(flag_rows, batch_points, block_size):
    batches, block_count = flag_rows.shape
    expanded = jnp.broadcast_to(
        flag_rows[:, None, :, None], (batches, batch_points, block_count, block_size)
    )
    return expanded.reshape(batches * batch_points, block_count * block_size)


def shards(
    point_values,
    sig_blocks,
    density,
    coulomb_core,
    screen_mask,
    ao_centers,
    ao_widths,
    point_coords,
    lmo_coeffs,
    domain_blocks,
):
    grid_count = lax.axis_size("grid")
    panel_index = lax.axis_index("tile")
    batches = sig_blocks.shape[0]
    own_rows, own_cols = density.shape
    points = point_values.shape[0]
    batch_points = points // batches
    block_size = coulomb_core.shape[0]
    total_aos = ao_widths.shape[0]
    all_blocks = total_aos // block_size
    col_blocks = own_cols // block_size
    row_blocks = own_rows // block_size
    block_ids = jnp.arange(all_blocks, dtype=jnp.int32)
    named_blocks = jnp.any(sig_blocks[:, :, None] == block_ids[None, None, :], axis=1).astype(
        jnp.float32
    )
    first_col = panel_index * col_blocks
    named_cols = lax.dynamic_slice_in_dim(named_blocks, first_col, col_blocks, 1)
    col_mask = spread_mask(named_cols, batch_points, block_size)
    masked_local = point_values * col_mask.astype(jnp.bfloat16)
    dest_named = jnp.max(named_blocks.reshape(batches, grid_count, row_blocks), axis=2)
    outgoing = masked_local.reshape(batches, batch_points, 1, own_cols) * dest_named[
        :, None, :, None
    ].astype(jnp.bfloat16)
    product = jnp.einsum(
        "bpgc,rc->bpgr",
        lax.all_to_all(outgoing, "grid", split_axis=2, concat_axis=2, tiled=True),
        density,
        preferred_element_type=jnp.float32,
    )
    arrivals = lax.all_to_all(
        product.astype(jnp.bfloat16), "grid", split_axis=2, concat_axis=2, tiled=True
    )
    row_mask = spread_mask(named_blocks, batch_points, block_size)
    partial_term = arrivals.reshape(points, total_aos).astype(jnp.float32) * row_mask
    coefficient = kernel_weights(ao_centers, ao_widths, point_coords)
    core_float = coulomb_core.astype(jnp.float32)
    screen_float = screen_mask.astype(jnp.float32)
    density_term = lax.psum(partial_term.astype(jnp.bfloat16), "tile").astype(jnp.float32)
    weighted = (coefficient * density_term).reshape(points, all_blocks, block_size)
    screen_rows = lax.dynamic_slice_in_dim(screen_float, first_col, col_blocks, 0)
    screened = jnp.einsum("kj,pja->pka", screen_rows, weighted, precision=highest)
    kernel_part = jnp.einsum(
        "ab,pkb->pka", core_float, screened, preferred_element_type=jnp.float32
    ).reshape(points, own_cols)
    coeff_cols = lax.dynamic_slice_in_dim(coefficient, panel_index * own_cols, own_cols, 1)
    potential = (coeff_cols * kernel_part * col_mask).astype(jnp.bfloat16)
    potential_out = jnp.broadcast_to(
        potential.reshape(batches, batch_points, 1, own_cols),
        (batches, batch_points, grid_count, own_cols),
    )
    whole_points = lax.all_gather(masked_local, "tile", axis=1, tiled=True)
    row_values, col_values = (
        lax.all_to_all(
            whole_points.reshape(batches, batch_points, grid_count, own_rows),
            "grid",
            split_axis=2,
            concat_axis=2,
            tiled=True,
        ),
        lax.all_to_all(potential_out, "grid", split_axis=2, concat_axis=2, tiled=True),
    )
    exch_tile = jnp.einsum(
        "bpgr,bpgc->rc", row_values, col_values, preferred_element_type=jnp.float32
    ).astype(jnp.bfloat16)
    number_of_slabs = domain_blocks.shape[0]
    localized_orbital_total = lmo_coeffs.shape[1]
    strip_width = localized_orbital_total // number_of_slabs
    local_ids = first_col + jnp.arange(col_blocks, dtype=jnp.int32)
    in_domain = jnp.any(domain_blocks[:, :, None] == local_ids[None, None, :], axis=1)
    domain_flags = jnp.transpose(in_domain)
    domain_mask = jnp.broadcast_to(
        domain_flags[:, None, :, None], (col_blocks, block_size, number_of_slabs, strip_width)
    ).reshape(own_cols, localized_orbital_total)
    region_expansion_factor = lmo_coeffs * domain_mask.astype(jnp.bfloat16)
    return lax.psum_scatter(
        lax.dot_general(
            region_expansion_factor,
            exch_tile,
            (((0,), (1,)), ((), ())),
            preferred_element_type=jnp.float32,
        ).astype(jnp.bfloat16),
        "tile",
        scatter_dimension=0,
        tiled=True,
    )


def solution(mesh):
    in_specs = (
        P("grid", "tile"),
        P("grid", None),
        P("grid", "tile"),
        P(),
        P(),
        P(),
        P(),
        P(None, "grid"),
        P("tile", None),
        P(),
    )
    out_specs = P("tile", "grid")
    return jax.shard_map(shards, mesh=mesh, in_specs=in_specs, out_specs=out_specs, check_vma=False)
```

profile of v0, /device:TPU:0, one launch (start us, length us, event | category | flops | bytes accessed | tf_op | source)
XLA Modules:
  0.0 288.2 jit_solution(9041671634119760462)
XLA Ops:
  6.5 0.0 copy-start
  6.5 0.8 fusion.26
  7.3 0.1 reshape.142
  7.4 0.1 dynamic-slice.3
  7.5 0.1 broadcast_bitcast_fusion.1
  7.6 0.1 reduce_max.9
  7.7 1.0 broadcast_multiply_fusion.1
  8.7 0.0 copy-start.2
  8.7 0.2 broadcast_multiply_fusion
  8.9 55.3 %all_to_all.20 = bf16[1,32,8,4096]{3,1,0,2:T(8,128)(2,1)S(1)} all-to-all(bf16[1,32,8,4096]{3,1,0,2:T(8,128)(2,1)S(1)} %broadcast_multiply_fusion), channel_id=1, replica_groups=mesh['grid'=8,'tile'=4] {'grid'}, dimensions={2} | all-to-all | bytes 4194304 | tf_op jit(solution)/shard_map/all_to_all | solution.py:59
  64.3 0.0 copy-done.2
  64.3 9.6 %fusion.11 = bf16[1,32,8,2048]{3,2,1,0:T(8,128)(2,1)} fusion(bf16[2048,4096]{1,0:T(8,128)(2,1)} %param.12, bf16[1,32,8,4096]{3,1,0,2:T(8,128)(2,1)S(1)} %all_to_all.20), kind=kOutput, calls=%fused_computation.9 | convolution fusion | flops 4295491584 | bytes 19922944 | tf_op jit(solution)/shard_map/bpgc,rc->bpgr/dot_general | solution.py:57
  73.8 2.8 copy.25
  76.6 3.6 %all-to-all-start.2 = ((bf16[1,32,8,2048]{3,1,0,2:T(8,128)(2,1)}), bf16[1,32,8,2048]{3,1,0,2:T(8,128)(2,1)S(1)}, u32[]{:S(2)}, u32[]{:S(2)}) async-start(bf16[1,32,8,2048]{3,1,0,2:T(8,128)(2,1)} %copy.25), calls=%async_computation.2 | async-start | bytes 2097152 | tf_op jit(solution)/shard_map/all_to_all | solution.py:63
  80.2 0.0 all-gather.2.cloned.1.call-start
  80.2 0.7 all-gather.2.cloned.1.call-update
  80.9 0.0 all-reduce.2.cloned.1.call-start
  81.0 0.1 broadcast_bitcast_fusion
  81.1 24.7 %all-to-all-done.2 = bf16[1,32,8,2048]{3,1,0,2:T(8,128)(2,1)S(1)} async-done(((bf16[1,32,8,2048]{3,1,0,2:T(8,128)(2,1)}), bf16[1,32,8,2048]{3,1,0,2:T(8,128)(2,1)S(1)}, u32[]{:S(2)}, u32[]{:S(2)}) %all-to-all-start.2) | async-done | bytes 1048608 | tf_op jit(solution)/shard_map/all_to_all | solution.py:63
  105.8 0.2 copy.31
  106.0 0.0 copy-start.3
  106.0 0.0 copy-start.6
  106.0 1.1 multiply_convert_fusion
  107.2 0.0 all-reduce.2.cloned.1.call-update
  107.2 0.0 copy-done.3
  107.2 0.0 copy-done.6
  107.2 0.8 multiply_reduce_fusion
  108.0 0.0 all-gather.2.cloned.1.call-done
  108.0 1.8 copy.30
  109.8 0.0 copy-start.4
  109.9 1.6 copy.22
  111.5 4.2 %all-to-all-start = ((bf16[1,32,8,2048]{3,1,0,2:T(8,128)(2,1)}), bf16[1,32,8,2048]{3,1,0,2:T(8,128)(2,1)}, u32[]{:S(2)}, u32[]{:S(2)}) async-start(bf16[1,32,8,2048]{3,1,0,2:T(8,128)(2,1)} %copy.22), calls=%async_computation | async-start | bytes 2097152 | tf_op jit(solution)/shard_map/all_to_all | solution.py:86
  115.7 26.8 %all-reduce.2.cloned.1.call-done = bf16[32,16384]{1,0:T(8,128)(2,1)} async-done(((bf16[32,16384]{1,0:T(8,128)(2,1)}), bf16[32,16384]{1,0:T(8,128)(2,1)}) %all-reduce.2.cloned.1.call-update) | async-done | bytes 1048592 | tf_op jit(solution)/shard_map/psum | solution.py:71
  142.5 0.0 copy-done.4
  142.5 1.5 convert_multiply_fusion
  144.0 1.2 copy.33
  145.2 1.9 convolution_bitcast_fusion
  147.1 0.0 copy-done
  147.1 0.3 fusion.24
  147.5 0.3 copy.34
  147.8 0.1 multiply_convert_fusion.1
  147.9 0.0 all-to-all-done
  147.9 1.6 broadcast_in_dim.49
  149.5 0.0 copy-start.5
  149.5 5.9 %all-to-all-start.3 = ((bf16[1,32,8,4096]{3,1,0,2:T(8,128)(2,1)}), bf16[1,32,8,4096]{3,1,0,2:T(8,128)(2,1)S(1)}, u32[]{:S(2)}, u32[]{:S(2)}) async-start(bf16[1,32,8,4096]{3,1,0,2:T(8,128)(2,1)} %broadcast_in_dim.49), calls=%async_computation.3 | async-start | bytes 4194304 | tf_op jit(solution)/shard_map/all_to_all | solution.py:93
  155.4 0.2 reduce-scatter.2.cloned.1.call-start
  155.6 0.0 copy-done.5
  155.7 0.2 compare_reduce_fusion
  155.9 0.1 copy.21
  156.0 2.2 broadcast_in_dim.18
  158.2 4.0 %copy.28 = pred[512,8,4,256]{3,1,2,0:T(8,128)(4,1)} copy(pred[512,8,4,256]{3,2,1,0:T(4,128)(4,1)S(1)} %bitcast.72) | data formatting | bytes 8388608
  162.3 40.5 %all-to-all-done.3 = bf16[1,32,8,4096]{3,1,0,2:T(8,128)(2,1)S(1)} async-done(((bf16[1,32,8,4096]{3,1,0,2:T(8,128)(2,1)}), bf16[1,32,8,4096]{3,1,0,2:T(8,128)(2,1)S(1)}, u32[]{:S(2)}, u32[]{:S(2)}) %all-to-all-start.3) | async-done | bytes 2097184 | tf_op jit(solution)/shard_map/all_to_all | solution.py:93
  202.8 10.0 %bitcast_convert_fusion.clone.7 = bf16[2048,4096]{1,0:T(8,128)(2,1)} fusion(bf16[1,32,8,4096]{3,1,0,2:T(8,128)(2,1)S(1)} %all-to-all-done.3, bf16[1,32,8,2048]{3,1,0,2:T(8,128)(2,1)} %all-to-all-done), kind=kOutput, calls=%fused_computation.clone.clone.clone.clone.clone.2 | convolution fusion | flops 4303355904 | bytes 19922944 | tf_op jit(solution)/shard_map/bpgr,bpgc->rc/dot_general | solution.py:95
  212.8 25.2 %fusion.5 = bf16[1024,2048]{1,0:T(8,128)(2,1)} fusion(pred[4096,1024]{1,0:T(8,128)(4,1)} %bitcast.77, bf16[4096,1024]{1,0:T(8,128)(2,1)} %param.18, bf16[2048,4096]{1,0:T(8,128)(2,1)} %bitcast_convert_fusion.clone.7), kind=kOutput, calls=%fused_computation.7 | convolution fusion | flops 17186160640 | bytes 33554432 | tf_op jit(solution)/shard_map/dot_general | solution.py:109
  237.9 0.0 copy-start.1
  237.9 0.0 reduce-scatter.2.cloned.1.call-update
  237.9 43.7 %reduce-scatter.2.cloned.1.call-done = bf16[256,2048]{1,0:T(8,128)(2,1)} async-done(((bf16[1024,2048]{1,0:T(8,128)(2,1)}), bf16[256,2048]{1,0:T(8,128)(2,1)}) %reduce-scatter.2.cloned.1.call-update) | async-done | bytes 1048592 | tf_op jit(solution)/shard_map/reduce_scatter | solution.py:108
  281.6 0.0 copy-done.1
  (5 shorter events, 0.0 us)
Async XLA Ops:
  6.5 140.6 %copy-start = (bf16[512,512]{1,0:T(8,128)(2,1)S(1)}, bf16[512,512]{1,0:T(8,128)(2,1)}, u32[]{:S(2)}) copy-start(bf16[512,512]{1,0:T(8,128)(2,1)} %param.13) | copy-start | bytes 1572868
  8.7 55.6 %copy-start.2 = (bf16[32,4096]{1,0:T(8,128)(2,1)}, bf16[32,4096]{1,0:T(8,128)(2,1)S(1)}, u32[]{:S(2)}) copy-start(bf16[32,4096]{1,0:T(8,128)(2,1)S(1)} %broadcast_multiply_fusion.1) | copy-start | bytes 786436
  76.6 29.2 %all-to-all-start.2 = ((bf16[1,32,8,2048]{3,1,0,2:T(8,128)(2,1)}), bf16[1,32,8,2048]{3,1,0,2:T(8,128)(2,1)S(1)}, u32[]{:S(2)}, u32[]{:S(2)}) async-start(bf16[1,32,8,2048]{3,1,0,2:T(8,128)(2,1)} %copy.25), calls=%async_computation.2 | async-start | bytes 2097152 | tf_op jit(solution)/shard_map/all_to_all | solution.py:63
  80.2 27.8 %all-gather.2.cloned.1.call-start = ((), (), s32[]{:S(2)}) async-start(), calls=%async_computation.5 | async-start | bytes 1310720 | tf_op jit(solution)/shard_map/all_gather | solution.py:84
  80.9 61.6 %all-reduce.2.cloned.1.call-start = ((), (), s32[]{:S(2)}) async-start(), calls=%async_computation.6 | async-start | bytes 2097152 | tf_op jit(solution)/shard_map/psum | solution.py:71
  106.0 1.2 copy-start.3
  106.0 1.2 copy-start.6
  109.8 32.6 %copy-start.4 = (f32[16384]{0:T(1024)S(1)}, f32[16384]{0:T(1024)}, u32[]{:S(2)}) copy-start(f32[16384]{0:T(1024)} %param.16) | copy-start | bytes 196612
  111.5 36.4 %all-to-all-start = ((bf16[1,32,8,2048]{3,1,0,2:T(8,128)(2,1)}), bf16[1,32,8,2048]{3,1,0,2:T(8,128)(2,1)}, u32[]{:S(2)}, u32[]{:S(2)}) async-start(bf16[1,32,8,2048]{3,1,0,2:T(8,128)(2,1)} %copy.22), calls=%async_computation | async-start | bytes 2097152 | tf_op jit(solution)/shard_map/all_to_all | solution.py:86
  149.5 6.2 %copy-start.5 = (s32[4,16]{1,0:T(4,128)S(1)}, s32[4,16]{1,0:T(4,128)}, u32[]{:S(2)}) copy-start(s32[4,16]{1,0:T(4,128)} %param.19) | copy-start | bytes 772
  149.5 53.3 %all-to-all-start.3 = ((bf16[1,32,8,4096]{3,1,0,2:T(8,128)(2,1)}), bf16[1,32,8,4096]{3,1,0,2:T(8,128)(2,1)S(1)}, u32[]{:S(2)}, u32[]{:S(2)}) async-start(bf16[1,32,8,4096]{3,1,0,2:T(8,128)(2,1)} %broadcast_in_dim.49), calls=%async_computation.3 | async-start | bytes 4194304 | tf_op jit(solution)/shard_map/all_to_all | solution.py:93
  155.4 126.2 %reduce-scatter.2.cloned.1.call-start = ((), (), s32[]{:S(2)}) async-start(), calls=%async_computation.7 | async-start | bytes 5242880 | tf_op jit(solution)/shard_map/reduce_scatter | solution.py:108
  237.9 43.7 %copy-start.1 = (bf16[512,512]{1,0:T(8,128)(2,1)S(1)}, bf16[512,512]{1,0:T(8,128)(2,1)}, u32[]{:S(2)}) copy-start(bf16[512,512]{1,0:T(8,128)(2,1)} %param.13) | copy-start | bytes 1572868
Sparse Core Ops, SparseCore 0:
  82.6 18.0 all-gather.1
  107.3 35.1 all-reduce.1
  238.1 43.5 reduce-scatter.1
where the time goes:
time: 289 us; the launch traced here: 288 us
  waiting for transfers between devices  136 us (47%)
  blocking collectives  55.3 us (19%)
  matrix products  46.9 us (16%)
  local copies, waits for them, and re-layouts  16.3 us (6%)
  starting transfers between devices  14 us (5%)
  between operations  13.3 us (5%)
  other arithmetic  5.85 us (2%)
    all_to_all x1, blocking collectives, shards(): lax.all_to_all(outgoing, 'grid', split_axis=2, concat_axis=2, tiled=True)  55.3 us
    reduce_scatter x1, waiting for transfers between devices, shards(): lax.psum_scatter(lax.dot_general(region_expansion_factor, exch_tile, (((0...  43.7 us
    all_to_all x1, waiting for transfers between devices, shards(): lax.all_to_all(potential_out, 'grid', split_axis=2, concat_axis=2, tiled=...  40.5 us
    psum x1, waiting for transfers between devices, shards(): lax.psum(partial_term.astype(jnp.bfloat16), 'tile').astype(jnp.float32)  26.8 us
    dot_general x1, matrix products, shards(): lax.dot_general(region_expansion_factor, exch_tile, (((0,), (1,)), ((), (...  25.2 us
    all_to_all x1, waiting for transfers between devices, shards(): lax.all_to_all(product.astype(jnp.bfloat16), 'grid', split_axis=2, concat...  24.7 us
    dot_general x1, matrix products, shards(): jnp.einsum('bpgr,bpgc->rc', row_values, col_values, preferred_element_typ...  9.96 us
    dot_general x1, matrix products, shards(): jnp.einsum('bpgc,rc->bpgr', lax.all_to_all(outgoing, 'grid', split_axis=2...  9.56 us
  transfers between devices with their start and end apart: 6, of which 4 were waited for; matrix products, arithmetic and copies ran while one was open for 6% of the time, Pallas kernels for 0%

commit v1 on v0

v1 whole, which is shorter than its diff:
```python
import functools
import math

import jax
import jax.numpy as jnp
from jax import lax
from jax.experimental import pallas as pl
from jax.experimental.pallas import tpu as pltpu
from jax.sharding import PartitionSpec as P

MESH = pl.DeviceIdType.MESH
VMEM_LIMIT = 60 * 1024 * 1024
f32 = jnp.float32
bf16 = jnp.bfloat16


def grid_split(grid_count):
    inner = max(1, math.isqrt(max(1, grid_count // 2)))
    while grid_count % inner:
        inner -= 1
    return grid_count // inner, inner


def tile_split(tile_count):
    inner = 2 if tile_count % 2 == 0 else 1
    return tile_count // inner, inner


def remote(src, dst, send_sem, recv_sem, device):
    return pltpu.make_async_remote_copy(
        src_ref=src,
        dst_ref=dst,
        send_sem=send_sem,
        recv_sem=recv_sem,
        device_id=device,
        device_id_type=MESH,
    )


def greet(devices):
    barrier = pltpu.get_barrier_semaphore()
    for device in devices:
        pl.semaphore_signal(barrier, inc=1, device_id=device, device_id_type=MESH)
    pl.semaphore_wait(barrier, len(devices))


def params(collective_id):
    return pltpu.CompilerParams(
        collective_id=collective_id, has_side_effects=True, vmem_limit_bytes=VMEM_LIMIT
    )


def vmem():
    return pl.BlockSpec(memory_space=pltpu.VMEM)


def spread_kernel(
    grid_count, tile_count, x_ref, all_ref, rows_ref, zs, zr, ys, yr, es, er, local_sem
):
    g, t = lax.axis_index("grid"), lax.axis_index("tile")
    nz, ny = grid_split(grid_count)
    z, y = g // ny, g % ny
    cols = x_ref.shape[1]
    rows = rows_ref.shape[2]
    offset = pl.multiple_of((g * rows) % cols, rows)
    owner = (g * rows) // cols == t

    z_peers = [(lax.rem(z + d, nz) * ny + y, t) for d in range(1, nz)]
    y_peers = [(z * ny + lax.rem(y + d, ny), t) for d in range(1, ny)]
    t_peers = [(g, lax.rem(t + d, tile_count)) for d in range(1, tile_count)]
    greet(z_peers + y_peers + t_peers)

    def z_source(dz):
        return lax.rem(z + nz - dz, nz)

    z_copies = [
        remote(x_ref, all_ref.at[g], zs.at[d], zr.at[d], z_peers[d]) for d in range(nz - 1)
    ]
    for copy in z_copies:
        copy.start()

    y_copies = {}

    def forward_y(dz):
        source = z_source(dz) * ny + y
        for d in range(ny - 1):
            block = x_ref if dz == 0 else all_ref.at[source]
            copy = remote(
                block, all_ref.at[source], ys.at[d, dz], yr.at[d, dz], y_peers[d]
            )
            copy.start()
            y_copies[d, dz] = copy

    def forward_rows(source, block):
        @pl.when(owner)
        def _():
            for d in range(tile_count - 1):
                remote(
                    block.at[:, pl.ds(offset, rows)],
                    rows_ref.at[source],
                    es.at[d],
                    er,
                    t_peers[d],
                ).start()

    forward_y(0)
    forward_rows(g, x_ref)
    keep = pltpu.make_async_copy(x_ref, all_ref.at[g], local_sem)
    keep.start()
    for dz in range(1, nz):
        source = z_source(dz) * ny + y
        z_copies[dz - 1].wait_recv()
        forward_y(dz)
        forward_rows(source, all_ref.at[source])
    for dz in range(nz):
        for d in range(ny - 1):
            source = z_source(dz) * ny + lax.rem(y + ny - d - 1, ny)
            y_copies[d, dz].wait_recv()
            forward_rows(source, all_ref.at[source])
    keep.wait()

    @pl.when(owner)
    def _():
        own = pltpu.make_async_copy(all_ref.at[:, :, pl.ds(offset, rows)], rows_ref, local_sem)
        own.start()
        for d in range(tile_count - 1):
            remote(rows_ref, rows_ref, es.at[d], er, t_peers[d]).wait_send()
        own.wait()

    @pl.when(jnp.logical_not(owner))
    def _():
        remote(rows_ref, rows_ref, es.at[0], er, t_peers[0]).wait_recv()

    for copy in z_copies:
        copy.wait_send()
    for copy in y_copies.values():
        copy.wait_send()


def spread(masked, grid_count, tile_count, rows):
    points, cols = masked.shape
    nz, ny = grid_split(grid_count)
    dma = pltpu.SemaphoreType.DMA
    return pl.pallas_call(
        functools.partial(spread_kernel, grid_count, tile_count),
        out_shape=(
            jax.ShapeDtypeStruct((grid_count, points, cols), bf16),
            jax.ShapeDtypeStruct((grid_count, points, rows), bf16),
        ),
        in_specs=[vmem()],
        out_specs=(vmem(), vmem()),
        scratch_shapes=[
            dma((nz,)),
            dma((nz,)),
            dma((ny, nz)),
            dma((ny, nz)),
            dma((tile_count,)),
            dma,
            dma,
        ],
        compiler_params=params(0),
    )(masked)


def reduce_kernel(
    grid_count,
    tile_count,
    part_ref,
    out_ref,
    sibling_ref,
    pair_ref,
    peer_ref,
    total_ref,
    cs,
    cr,
    xs,
    xr,
    gs,
    gr,
):
    g, t = lax.axis_index("grid"), lax.axis_index("tile")
    nx, nc = tile_split(tile_count)
    x, c = t // nc, t % nc
    sibling = 1 - c if nc == 2 else c
    x_peers = [(g, lax.rem(x + d, nx) * nc + c) for d in range(1, nx)]
    g_peers = [(lax.rem(g + d, grid_count), t) for d in range(1, grid_count)]
    c_peers = [(g, x * nc + sibling)] if nc == 2 else []
    greet(c_peers + x_peers + g_peers)

    c_copies = []
    if nc == 2:
        for d in range(nx):
            column = lax.rem(x + d, nx)
            c_copies.append(
                remote(
                    part_ref.at[:, column, sibling],
                    sibling_ref.at[:, column],
                    cs.at[d],
                    cr.at[d],
                    c_peers[0],
                )
            )
        order = list(range(1, nx)) + [0]
        for d in order:
            c_copies[d].start()

    def pair(d):
        column = lax.rem(x + d, nx)
        if nc == 2:
            c_copies[d].wait_recv()

        @pl.loop(0, grid_count)
        def _(i):
            value = part_ref[i, column, c].astype(f32)
            if nc == 2:
                value = value + sibling_ref[i, column].astype(f32)
            pair_ref[d, i] = value.astype(bf16)

    x_copies = []
    for d in range(1, nx):
        pair(d)
        copy = remote(
            pair_ref.at[d], peer_ref.at[d], xs.at[d], xr.at[d], x_peers[d - 1]
        )
        copy.start()
        x_copies.append(copy)
    pair(0)
    for copy in x_copies:
        copy.wait_recv()

    @pl.loop(0, grid_count)
    def _(i):
        value = pair_ref[0, i].astype(f32)
        for d in range(1, nx):
            value = value + peer_ref[d, i].astype(f32)
        total_ref[i] = value.astype(bf16)

    g_copies = []
    for d in range(1, grid_count):
        target = lax.rem(g + d, grid_count)
        copy = remote(
            total_ref.at[target], out_ref.at[g], gs.at[d], gr.at[d], g_peers[d - 1]
        )
        copy.start()
        g_copies.append(copy)
    out_ref[g] = total_ref[g]
    for copy in c_copies:
        copy.wait_send()
    for copy in x_copies:
        copy.wait_send()
    for copy in g_copies:
        copy.wait()


def reduce_parts(parts, grid_count, tile_count):
    nx, nc = tile_split(tile_count)
    points, rows = parts.shape
    slab = points // (grid_count * tile_count)
    dma = pltpu.SemaphoreType.DMA
    return pl.pallas_call(
        functools.partial(reduce_kernel, grid_count, tile_count),
        out_shape=jax.ShapeDtypeStruct((grid_count, slab, rows), bf16),
        in_specs=[vmem()],
        out_specs=vmem(),
        scratch_shapes=[
            pltpu.VMEM((grid_count, nx, slab, rows), bf16),
            pltpu.VMEM((nx, grid_count, slab, rows), bf16),
            pltpu.VMEM((nx, grid_count, slab, rows), bf16),
            pltpu.VMEM((grid_count, slab, rows), bf16),
            dma((nx,)),
            dma((nx,)),
            dma((nx,)),
            dma((nx,)),
            dma((grid_count,)),
            dma((grid_count,)),
        ],
        compiler_params=params(1),
    )(parts.reshape(grid_count, nx, nc, slab, rows))


def finish_kernel(
    grid_count,
    tile_count,
    pot_ref,
    lmo_hbm,
    mask_ref,
    rows_ref,
    out_ref,
    lmo_ref,
    got_ref,
    flat_ref,
    send_ref,
    part_ref,
    own_ref,
    all_ref,
    lmo_sem,
    vs,
    vr,
    ws,
    wr,
    gs,
    gr,
):
    g, t = lax.axis_index("grid"), lax.axis_index("tile")
    load = pltpu.make_async_copy(lmo_hbm, lmo_ref, lmo_sem)
    load.start()
    t_peers = [(g, lax.rem(t + d, tile_count)) for d in range(1, tile_count)]
    g_peers = [(lax.rem(g + d, grid_count), t) for d in range(1, grid_count)]
    greet(t_peers + g_peers)
    cols = mask_ref.shape[0]
    slab = pot_ref.shape[1]
    block = pot_ref.shape[2]
    strip = own_ref.shape[1]

    v_copies = []
    for d in range(1, tile_count):
        target = lax.rem(t + d, tile_count)
        copy = remote(
            pot_ref.at[pl.ds(target * cols, cols)],
            got_ref.at[t],
            vs.at[d],
            vr.at[d],
            t_peers[d - 1],
        )
        copy.start()
        v_copies.append(copy)
    got_ref[t] = pot_ref[pl.ds(t * cols, cols)]
    for copy in v_copies:
        copy.wait()
    for i in range(tile_count):
        for m in range(cols):
            flat_ref[m, i * slab : (i + 1) * slab, :] = got_ref[i, m].astype(f32)
    load.wait()
    for s in range(tile_count):
        lanes = slice(s * strip, (s + 1) * strip)
        total = None
        for m in range(cols):
            term = mask_ref[m : m + 1, lanes] * jnp.dot(
                flat_ref[m].astype(bf16),
                lmo_ref[m * block : (m + 1) * block, lanes],
                preferred_element_type=f32,
            )
            total = term if total is None else total + term
        send_ref[s] = total.astype(bf16)
    w_copies = []
    for d in range(1, tile_count):
        target = lax.rem(t + d, tile_count)
        copy = remote(
            send_ref.at[target], part_ref.at[d], ws.at[d], wr.at[d], t_peers[d - 1]
        )
        copy.start()
        w_copies.append(copy)
    total = send_ref[t].astype(f32)
    for d, copy in enumerate(w_copies):
        copy.wait()
        total = total + part_ref[d + 1].astype(f32)
    own_ref[...] = total.astype(bf16)
    g_copies = []
    for d in range(1, grid_count):
        copy = remote(own_ref, all_ref.at[g], gs.at[d], gr.at[d], g_peers[d - 1])
        copy.start()
        g_copies.append(copy)
    all_ref[g] = own_ref[...]
    for copy in g_copies:
        copy.wait()
    points = grid_count * own_ref.shape[0]
    weights = all_ref[...].astype(f32).reshape(points, strip).T.astype(bf16)
    rows = out_ref.shape[1]
    step = min(rows, 512)
    for i in range(rows // step):
        lanes = slice(i * step, (i + 1) * step)
        out_ref[:, lanes] = jnp.dot(
            weights,
            rows_ref[:, :, lanes].reshape(points, step),
            preferred_element_type=f32,
        ).astype(bf16)


def finish(potential, lmo_coeffs, mask, rows, grid_count, tile_count):
    blocks, slab, block = potential.shape
    cols = blocks // tile_count
    total = lmo_coeffs.shape[1]
    strip = total // tile_count
    batch = rows.shape[1]
    dma = pltpu.SemaphoreType.DMA
    return pl.pallas_call(
        functools.partial(finish_kernel, grid_count, tile_count),
        out_shape=jax.ShapeDtypeStruct((strip, rows.shape[2]), bf16),
        in_specs=[vmem(), pl.BlockSpec(memory_space=pl.ANY), vmem(), vmem()],
        out_specs=vmem(),
        scratch_shapes=[
            pltpu.VMEM(lmo_coeffs.shape, bf16),
            pltpu.VMEM((tile_count, cols, slab, block), bf16),
            pltpu.VMEM((cols, batch, block), f32),
            pltpu.VMEM((tile_count, batch, strip), bf16),
            pltpu.VMEM((tile_count, batch, strip), bf16),
            pltpu.VMEM((batch, strip), bf16),
            pltpu.VMEM((grid_count, batch, strip), bf16),
            dma,
            dma((tile_count,)),
            dma((tile_count,)),
            dma((tile_count,)),
            dma((tile_count,)),
            dma((grid_count,)),
            dma((grid_count,)),
        ],
        compiler_params=params(2),
    )(potential, lmo_coeffs, mask, rows)


def shards(
    point_values,
    sig_blocks,
    density,
    coulomb_core,
    screen_mask,
    ao_centers,
    ao_widths,
    point_coords,
    lmo_coeffs,
    domain_blocks,
):
    grid_count = lax.axis_size("grid")
    tile_count = lax.axis_size("tile")
    panel = lax.axis_index("tile")
    own_rows, own_cols = density.shape
    points = point_values.shape[0]
    block_size = coulomb_core.shape[0]
    total_aos = ao_widths.shape[0]
    all_blocks = total_aos // block_size
    col_blocks = own_cols // block_size
    slab = points // tile_count
    block_ids = jnp.arange(all_blocks, dtype=jnp.int32)
    named = jnp.any(sig_blocks[0][:, None] == block_ids[None, :], axis=0)
    first_col = panel * col_blocks
    named_cols = lax.dynamic_slice_in_dim(named.astype(f32), first_col, col_blocks, 0)
    col_mask = jnp.repeat(named_cols, block_size)
    masked = point_values * col_mask[None, :].astype(bf16)
    all_values, row_values = spread(masked, grid_count, tile_count, own_rows)
    parts = lax.dot_general(
        all_values.reshape(grid_count * points, own_cols),
        density,
        (((1,), (1,)), ((), ())),
        preferred_element_type=f32,
    ).astype(bf16)
    summed = reduce_parts(parts, grid_count, tile_count)
    row_blocks = own_rows // block_size
    term = summed.astype(f32).reshape(grid_count, slab, row_blocks, block_size)
    term = jnp.transpose(term, (0, 2, 1, 3)).reshape(all_blocks, slab, block_size)
    coords = lax.dynamic_slice_in_dim(point_coords, panel * slab, slab, 1)
    offsets = (
        ao_centers.reshape(3, all_blocks, 1, block_size) - coords.reshape(3, 1, slab, 1)
    )
    coefficient = 1.0 / jnp.sqrt(
        jnp.sum(offsets * offsets, axis=0) + ao_widths.reshape(all_blocks, 1, block_size)
    )
    scaled = coefficient * named.astype(f32)[:, None, None]
    weighted = (scaled * term).astype(bf16)
    screened = jnp.einsum(
        "kj,jpa->kpa", screen_mask.astype(bf16), weighted, preferred_element_type=f32
    ).astype(bf16)
    mixed = jnp.einsum(
        "kpc,ac->kpa", screened, coulomb_core, preferred_element_type=f32
    )
    potential = (scaled * mixed).astype(bf16)
    local_ids = first_col + jnp.arange(col_blocks, dtype=jnp.int32)
    in_domain = jnp.any(domain_blocks[:, :, None] == local_ids[None, None, :], axis=1)
    strip_width = lmo_coeffs.shape[1] // domain_blocks.shape[0]
    mask = jnp.repeat(jnp.transpose(in_domain).astype(f32), strip_width, axis=1)
    return finish(potential, lmo_coeffs, mask, row_values, grid_count, tile_count)


def solution(mesh):
    in_specs = (
        P("grid", "tile"),
        P("grid", None),
        P("grid", "tile"),
        P(),
        P(),
        P(),
        P(),
        P(None, "grid"),
        P("tile", None),
        P(),
    )
    out_specs = P("tile", "grid")
    return jax.shard_map(shards, mesh=mesh, in_specs=in_specs, out_specs=out_specs, check_vma=False)
```

time: 289 us -> 108 us (0.37)
  waiting for transfers between devices: 136 us -> 0 us
  Pallas kernels: 0 us -> 86.8 us
  blocking collectives: 55.3 us -> 0 us
  matrix products: 46.9 us -> 13.2 us
  starting transfers between devices: 14 us -> 0 us
  between operations: 13.3 us -> 0.12 us
  local copies, waits for them, and re-layouts: 16.3 us -> 4.4 us
    pallas_call x0 -> x3, Pallas kernels: none -> 86.8 us  [the longest x1 44.9 us: spread(): pl.pallas_call(functools.partial(spread_kernel, grid_count, tile_count),...]
    all_to_all x3 -> x0, waiting for transfers between devices: 65.2 us -> none  [the longest x1 40.5 us: shards(): lax.all_to_all(potential_out, 'grid', split_axis=2, concat_axis=2, tiled=...]
    all_to_all x1 -> x0, blocking collectives: 55.3 us -> none  [shards(): lax.all_to_all(outgoing, 'grid', split_axis=2, concat_axis=2, tiled=True)]
    reduce_scatter x1 -> x0, waiting for transfers between devices: 43.7 us -> none  [shards(): lax.psum_scatter(lax.dot_general(region_expansion_factor, exch_tile, (((0...]
    dot_general x5 -> x3, matrix products: 46.9 us -> 13.2 us  [the longest x1 11.9 us: shards(): lax.dot_general(all_values.reshape(grid_count * points, own_cols), densit...]
    psum x1 -> x0, waiting for transfers between devices: 26.8 us -> none  [shards(): lax.psum(partial_term.astype(jnp.bfloat16), 'tile').astype(jnp.float32)]
    all_to_all x3 -> x0, starting transfers between devices: 13.8 us -> none  [the longest x1 5.94 us: shards(): lax.all_to_all(potential_out, 'grid', split_axis=2, concat_axis=2, tiled=...]
    unnamed x23 -> x16, local copies, waits for them, and re-layouts: 7.83 us -> 2.56 us
  transfers between devices with their start and end apart: 6 -> 0, of which waited for: 4 -> 0; matrix products, arithmetic and copies ran while one was open for 6% -> 0% of each run, Pallas kernels for 0% -> 0%
where the time goes in v1:
time: 108 us
  Pallas kernels  86.8 us (80%)
  matrix products  13.2 us (12%)
  local copies, waits for them, and re-layouts  4.4 us (4%)
  other arithmetic  3.12 us (3%)
    pallas_call x1, Pallas kernels, spread(): pl.pallas_call(functools.partial(spread_kernel, grid_count, tile_count),...  44.9 us
    pallas_call x1, Pallas kernels, reduce_parts(): pl.pallas_call(functools.partial(reduce_kernel, grid_count, tile_count),...  22.4 us
    pallas_call x1, Pallas kernels, finish(): pl.pallas_call(functools.partial(finish_kernel, grid_count, tile_count),...  19.4 us
    dot_general x1, matrix products, shards(): lax.dot_general(all_values.reshape(grid_count * points, own_cols), densit...  11.9 us
    unnamed x16, local copies, waits for them, and re-layouts  2.56 us

profile of v1, /device:TPU:0, one launch (start us, length us, event | category | flops | bytes accessed | tf_op | source)
XLA Modules:
  0.0 107.6 jit_solution(16898597002290449745)
XLA Ops:
  0.0 0.0 copy-start
  0.0 0.8 fusion.8
  0.8 0.1 dynamic_slice.10
  0.9 0.1 broadcast_bitcast_fusion
  1.0 1.7 %broadcast_multiply_fusion.x_ref = bf16[32,4096]{1,0:T(8,128)(2,1)} fusion(bf16[32,4096]{1,0:T(8,128)(2,1)} %param.10, bf16[4096]{0:T(1024)(128)(2,1)S(1)} %bitcast.30), kind=kLoop, calls=%fused_computation.13 | loop fusion | flops 131072 | bytes 532480 | tf_op jit(solution)/shard_map/mul | solution.py:438
  2.7 44.9 %shard_map.100 = (bf16[8,32,4096]{2,1,0:T(8,128)(2,1)}, bf16[8,32,2048]{2,1,0:T(8,128)(2,1)}) custom-call(bf16[32,4096]{1,0:T(8,128)(2,1)} %broadcast_multiply_fusion.x_ref), custom_call_target="tpu_custom_call" | custom-call | tf_op jit(solution)/shard_map/pallas_call | solution.py:144
  47.6 11.9 %convolution_convert_fusion = bf16[256,2048]{1,0:T(8,128)(2,1)} fusion(bf16[256,4096]{1,0:T(8,128)(2,1)} %bitcast.31, bf16[2048,4096]{1,0:T(8,128)(2,1)} %param.12), kind=kOutput, calls=%fused_computation | convolution fusion | flops 4295491584 | bytes 19922944 | tf_op jit(solution)/shard_map/dot_general | solution.py:440
  59.5 0.0 copy-start.5
  59.5 0.0 copy-start.1
  59.5 0.0 copy-start.2
  59.5 22.4 %shard_map.101 = bf16[8,8,2048]{2,1,0:T(8,128)(2,1)} custom-call(bf16[8,2,2,8,2048]{4,3,2,1,0:T(8,128)(2,1)} %bitcast.26), custom_call_target="tpu_custom_call" | custom-call | tf_op jit(solution)/shard_map/pallas_call | solution.py:260
  81.9 1.0 fusion.9
  82.9 0.0 copy-start.3
  83.0 0.0 copy-done.5
  83.0 0.1 constant_dynamic-slice_fusion
  83.1 0.0 copy-done.1
  83.1 0.1 copy.22
  83.1 0.0 copy-start.4
  83.1 0.2 multiply_reduce_fusion
  83.4 0.0 copy-done.2
  83.4 0.1 multiply_convert_fusion
  83.6 0.1 copy-done.3
  83.6 0.2 fusion.4
  83.9 0.0 copy-done
  83.9 1.1 fusion.pot_ref
  84.9 0.0 copy-done.4
  84.9 0.2 compare_reduce_fusion
  85.2 0.7 broadcast_in_dim.5
  85.8 19.4 %shard_map.102 = bf16[256,2048]{1,0:T(8,128)(2,1)} custom-call(bf16[32,8,512]{2,1,0:T(8,128)(2,1)} %fusion.pot_ref, bf16[4096,1024]{1,0:T(8,128)(2,1)} %lmo_hbm.1, f32[8,1024]{1,0:T(8,128)} %bitcast.29, bf16[8,32,2048]{2,1,0:T(8,128)(2,1)} %get-tuple-element.8.rows_ref), custom_call_target="tpu_custom_call" | custom-call | tf_op jit(solution)/shard_map/pallas_call | solution.py:386
  105.3 2.3 %copy.24 = bf16[256,2048]{1,0:T(8,128)(2,1)} copy(bf16[256,2048]{1,0:T(8,128)(2,1)} %shard_map.102) | data formatting | bytes 2097152
  (6 shorter events, 0.1 us)
Async XLA Ops:
  0.0 83.9 %copy-start = (bf16[512,512]{1,0:T(8,128)(2,1)S(1)}, bf16[512,512]{1,0:T(8,128)(2,1)}, u32[]{:S(2)}) copy-start(bf16[512,512]{1,0:T(8,128)(2,1)} %param.13) | copy-start | bytes 1572868
  59.5 23.5 %copy-start.5 = (f32[3,32]{1,0:T(4,128)S(1)}, f32[3,32]{1,0:T(4,128)}, u32[]{:S(2)}) copy-start(f32[3,32]{1,0:T(4,128)} %param.17) | copy-start | bytes 1156
  59.5 23.6 %copy-start.1 = (f32[3,16384]{1,0:T(4,128)S(1)}, f32[3,16384]{1,0:T(4,128)}, u32[]{:S(2)}) copy-start(f32[3,16384]{1,0:T(4,128)} %param.15) | copy-start | bytes 589828
  59.5 23.9 %copy-start.2 = (f32[16384]{0:T(1024)S(1)}, f32[16384]{0:T(1024)}, u32[]{:S(2)}) copy-start(f32[16384]{0:T(1024)} %param.16) | copy-start | bytes 196612
  82.9 0.7 copy-start.3
  83.1 1.8 %copy-start.4 = (s32[4,16]{1,0:T(4,128)S(1)}, s32[4,16]{1,0:T(4,128)}, u32[]{:S(2)}) copy-start(s32[4,16]{1,0:T(4,128)} %param.19) | copy-start | bytes 772

commit v2 on v1

--- a/solution.py
+++ b/solution.py
@@ -59,87 +59,179 @@
 ):
     g, t = lax.axis_index("grid"), lax.axis_index("tile")
     nz, ny = grid_split(grid_count)
+    nx, nc = tile_split(tile_count)
     z, y = g // ny, g % ny
+    x, c = t // nc, t % nc
     cols = x_ref.shape[1]
     rows = rows_ref.shape[2]
     offset = pl.multiple_of((g * rows) % cols, rows)
-    owner = (g * rows) // cols == t
-
-    z_peers = [(lax.rem(z + d, nz) * ny + y, t) for d in range(1, nz)]
+    owner = (g * rows) // cols
+    is_owner = owner == t
+    in_column = owner % nc == c
+    has_left, has_right = z > 0, z < nz - 1
+    left = (lax.rem(z + nz - 1, nz) * ny + y, t)
+    right = (lax.rem(z + 1, nz) * ny + y, t)
     y_peers = [(z * ny + lax.rem(y + d, ny), t) for d in range(1, ny)]
-    t_peers = [(g, lax.rem(t + d, tile_count)) for d in range(1, tile_count)]
-    greet(z_peers + y_peers + t_peers)
-
-    def z_source(dz):
-        return lax.rem(z + nz - dz, nz)
-
-    z_copies = [
-        remote(x_ref, all_ref.at[g], zs.at[d], zr.at[d], z_peers[d]) for d in range(nz - 1)
-    ]
-    for copy in z_copies:
-        copy.start()
-
-    y_copies = {}
-
-    def forward_y(dz):
-        source = z_source(dz) * ny + y
-        for d in range(ny - 1):
-            block = x_ref if dz == 0 else all_ref.at[source]
-            copy = remote(
-                block, all_ref.at[source], ys.at[d, dz], yr.at[d, dz], y_peers[d]
-            )
-            copy.start()
-            y_copies[d, dz] = copy
-
-    def forward_rows(source, block):
-        @pl.when(owner)
+    x_peers = [(g, lax.rem(x + d, nx) * nc + c) for d in range(1, nx)]
+    c_peers = [(g, x * nc + (1 - c))] if nc == 2 else []
+    greet([left, right] + y_peers + x_peers + c_peers)
+
+    def present(k):
+        if k == 0:
+            return z >= 0
+        step = (k + 1) // 2
+        return z >= step if k % 2 else z <= nz - 1 - step
+
+    def source(k, d):
+        step = (k + 1) // 2
+        line = lax.rem(z + nz - step, nz) if k % 2 else lax.rem(z + step, nz)
+        return line * ny + lax.rem(y + ny - d, ny)
+
+    def block(k, d):
+        return x_ref if k == 0 and d == 0 else all_ref.at[source(k, d)]
+
+    def along(k, to_right):
+        step = (k + 1) // 2
+        lane = 0 if to_right else 1
+        return remote(
+            block(k, 0),
+            all_ref.at[source(k, 0)],
+            zs.at[lane, step],
+            zr.at[lane, step],
+            right if to_right else left,
+        )
+
+    def across(k, d):
+        return remote(
+            block(k, 0), all_ref.at[source(k, 0)], ys.at[d, k], yr.at[d, k], y_peers[d - 1]
+        )
+
+    def arrived(k, d, sends, recvs):
+        spot = all_ref.at[source(k, d)]
+        remote(spot, spot, sends, recvs, right).wait_recv()
+
+    def share(k, d):
+        for i, peer in enumerate(x_peers + c_peers):
+            remote(
+                block(k, d).at[:, pl.ds(offset, rows)],
+                rows_ref.at[source(k, d)],
+                es.at[i],
+                er.at[d, k],
+                peer,
+            ).start()
+
+    steps = range(2 * nz - 1)
+
+    def send_block(k):
+        if k == 0 or k % 2:
+
+            @pl.when(has_right)
+            def _():
+                along(k, True).start()
+
+        if k == 0 or k % 2 == 0:
+
+            @pl.when(has_left)
+            def _():
+                along(k, False).start()
+
+        for d in range(1, ny):
+            across(k, d).start()
+
+        @pl.when(is_owner)
         def _():
-            for d in range(tile_count - 1):
-                remote(
-                    block.at[:, pl.ds(offset, rows)],
-                    rows_ref.at[source],
-                    es.at[d],
-                    er,
-                    t_peers[d],
-                ).start()
-
-    forward_y(0)
-    forward_rows(g, x_ref)
+            share(k, 0)
+
+    def take_across(k):
+        @pl.when(present(k))
+        def _():
+            for d in range(1, ny):
+                arrived(k, d, ys.at[d, k], yr.at[d, k])
+
+                @pl.when(is_owner)
+                def _():
+                    share(k, d)
+
+    send_block(0)
     keep = pltpu.make_async_copy(x_ref, all_ref.at[g], local_sem)
     keep.start()
-    for dz in range(1, nz):
-        source = z_source(dz) * ny + y
-        z_copies[dz - 1].wait_recv()
-        forward_y(dz)
-        forward_rows(source, all_ref.at[source])
-    for dz in range(nz):
-        for d in range(ny - 1):
-            source = z_source(dz) * ny + lax.rem(y + ny - d - 1, ny)
-            y_copies[d, dz].wait_recv()
-            forward_rows(source, all_ref.at[source])
+    for step in range(1, nz):
+        for k in (2 * step - 1, 2 * step):
+
+            @pl.when(present(k))
+            def _():
+                lane = 0 if k % 2 else 1
+                arrived(k, 0, zs.at[lane, step - 1], zr.at[lane, step - 1])
+                send_block(k)
+
+        if step == 1:
+            take_across(0)
+        else:
+            take_across(2 * step - 3)
+            take_across(2 * step - 2)
+    if nz > 1:
+        take_across(2 * nz - 3)
+        take_across(2 * nz - 2)
+    else:
+        take_across(0)
     keep.wait()
 
-    @pl.when(owner)
+    @pl.when(is_owner)
     def _():
         own = pltpu.make_async_copy(all_ref.at[:, :, pl.ds(offset, rows)], rows_ref, local_sem)
         own.start()
-        for d in range(tile_count - 1):
-            remote(rows_ref, rows_ref, es.at[d], er, t_peers[d]).wait_send()
+        for i in range(len(x_peers + c_peers)):
+            remote(rows_ref, rows_ref, es.at[i], er.at[0, 0], right).wait_send()
         own.wait()
 
-    @pl.when(jnp.logical_not(owner))
+    @pl.when(jnp.logical_not(is_owner))
     def _():
-        remote(rows_ref, rows_ref, es.at[0], er, t_peers[0]).wait_recv()
-
-    for copy in z_copies:
-        copy.wait_send()
-    for copy in y_copies.values():
-        copy.wait_send()
+        for k in steps:
+
+            @pl.when(present(k))
+            def _():
+                for d in range(ny):
+                    spot = rows_ref.at[source(k, d)]
+                    pass_on = remote(
+                        spot, spot, es.at[nx - 1], er.at[d, k], (c_peers or [right])[0]
+                    )
+                    pass_on.wait_recv()
+                    if nc == 2:
+
+                        @pl.when(in_column)
+                        def _():
+                            pass_on.start()
+
+        if nc == 2:
+
+            @pl.when(in_column)
+            def _():
+                remote(rows_ref, rows_ref, es.at[nx - 1], er.at[0, 0], right).wait_send()
+
+    for k in steps:
+
+        @pl.when(present(k))
+        def _():
+            if k == 0 or k % 2:
+
+                @pl.when(has_right)
+                def _():
+                    along(k, True).wait_send()
+
+            if k == 0 or k % 2 == 0:
+
+                @pl.when(has_left)
+                def _():
+                    along(k, False).wait_send()
+
+            for d in range(1, ny):
+                across(k, d).wait_send()
 
 
 def spread(masked, grid_count, tile_count, rows):
     points, cols = masked.shape
     nz, ny = grid_split(grid_count)
+    nx, nc = tile_split(tile_count)
     dma = pltpu.SemaphoreType.DMA
     return pl.pallas_call(
         functools.partial(spread_kernel, grid_count, tile_count),
@@ -150,12 +242,12 @@
         in_specs=[vmem()],
         out_specs=(vmem(), vmem()),
         scratch_shapes=[
-            dma((nz,)),
-            dma((nz,)),
-            dma((ny, nz)),
-            dma((ny, nz)),
-            dma((tile_count,)),
-            dma,
+            dma((2, nz)),
+            dma((2, nz)),
+            dma((ny, 2 * nz)),
+            dma((ny, 2 * nz)),
+            dma((nx,)),
+            dma((ny, 2 * nz)),
             dma,
         ],
         compiler_params=params(0),
@@ -284,15 +376,13 @@
     pot_ref,
     lmo_hbm,
     mask_ref,
-    rows_ref,
-    out_ref,
+    all_ref,
     lmo_ref,
     got_ref,
     flat_ref,
     send_ref,
     part_ref,
     own_ref,
-    all_ref,
     lmo_sem,
     vs,
     vr,
@@ -363,30 +453,18 @@
     all_ref[g] = own_ref[...]
     for copy in g_copies:
         copy.wait()
-    points = grid_count * own_ref.shape[0]
-    weights = all_ref[...].astype(f32).reshape(points, strip).T.astype(bf16)
-    rows = out_ref.shape[1]
-    step = min(rows, 512)
-    for i in range(rows // step):
-        lanes = slice(i * step, (i + 1) * step)
-        out_ref[:, lanes] = jnp.dot(
-            weights,
-            rows_ref[:, :, lanes].reshape(points, step),
-            preferred_element_type=f32,
-        ).astype(bf16)
-
-
-def finish(potential, lmo_coeffs, mask, rows, grid_count, tile_count):
+
+
+def finish(potential, lmo_coeffs, mask, batch, grid_count, tile_count):
     blocks, slab, block = potential.shape
     cols = blocks // tile_count
     total = lmo_coeffs.shape[1]
     strip = total // tile_count
-    batch = rows.shape[1]
     dma = pltpu.SemaphoreType.DMA
     return pl.pallas_call(
         functools.partial(finish_kernel, grid_count, tile_count),
-        out_shape=jax.ShapeDtypeStruct((strip, rows.shape[2]), bf16),
-        in_specs=[vmem(), pl.BlockSpec(memory_space=pl.ANY), vmem(), vmem()],
+        out_shape=jax.ShapeDtypeStruct((grid_count, batch, strip), bf16),
+        in_specs=[vmem(), pl.BlockSpec(memory_space=pl.ANY), vmem()],
         out_specs=vmem(),
         scratch_shapes=[
             pltpu.VMEM(lmo_coeffs.shape, bf16),
@@ -395,7 +473,6 @@
             pltpu.VMEM((tile_count, batch, strip), bf16),
             pltpu.VMEM((tile_count, batch, strip), bf16),
             pltpu.VMEM((batch, strip), bf16),
-            pltpu.VMEM((grid_count, batch, strip), bf16),
             dma,
             dma((tile_count,)),
             dma((tile_count,)),
@@ -405,7 +482,7 @@
             dma((grid_count,)),
         ],
         compiler_params=params(2),
-    )(potential, lmo_coeffs, mask, rows)
+    )(potential, lmo_coeffs, mask)
 
 
 def shards(
@@ -467,7 +544,13 @@
     in_domain = jnp.any(domain_blocks[:, :, None] == local_ids[None, None, :], axis=1)
     strip_width = lmo_coeffs.shape[1] // domain_blocks.shape[0]
     mask = jnp.repeat(jnp.transpose(in_domain).astype(f32), strip_width, axis=1)
-    return finish(potential, lmo_coeffs, mask, row_values, grid_count, tile_count)
+    weights = finish(potential, lmo_coeffs, mask, points, grid_count, tile_count)
+    return lax.dot_general(
+        weights.reshape(grid_count * points, weights.shape[2]),
+        row_values.reshape(grid_count * points, own_rows),
+        (((0,), (0,)), ((), ())),
+        preferred_element_type=f32,
+    ).astype(bf16)
 
 
 def solution(mesh):

time: 108 us -> 96.6 us (0.89)
  Pallas kernels: 86.8 us -> 75.4 us
  matrix products: 13.2 us -> 15.5 us
  local copies, waits for them, and re-layouts: 4.4 us -> 2.1 us
    pallas_call x1, Pallas kernels: 44.9 us -> 36.3 us  [spread(): pl.pallas_call(functools.partial(spread_kernel, grid_count, tile_count),...]
    pallas_call x1, Pallas kernels: 19.4 us -> 16.6 us  [finish(): pl.pallas_call(functools.partial(finish_kernel, grid_count, tile_count),...]
    dot_general x0 -> x1, matrix products: none -> 2.34 us  [shards(): lax.dot_general(weights.reshape(grid_count * points, weights.shape[2]), r...]
    unnamed x16 -> x17, local copies, waits for them, and re-layouts: 2.56 us -> 0.26 us
where the time goes in v2:
time: 96.6 us; the launch traced here: 96.3 us
  Pallas kernels  75.4 us (78%)
  matrix products  15.5 us (16%)
  other arithmetic  3.12 us (3%)
  local copies, waits for them, and re-layouts  2.1 us (2%)
    pallas_call x1, Pallas kernels, spread(): pl.pallas_call(functools.partial(spread_kernel, grid_count, tile_count),...  36.3 us
    pallas_call x1, Pallas kernels, reduce_parts(): pl.pallas_call(functools.partial(reduce_kernel, grid_count, tile_count),...  22.4 us
    pallas_call x1, Pallas kernels, finish(): pl.pallas_call(functools.partial(finish_kernel, grid_count, tile_count),...  16.6 us
    dot_general x1, matrix products, shards(): lax.dot_general(all_values.reshape(grid_count * points, own_cols), densit...  11.9 us
    dot_general x1, matrix products, shards(): lax.dot_general(weights.reshape(grid_count * points, weights.shape[2]), r...  2.34 us

profile of v2, /device:TPU:0, one launch (start us, length us, event | category | flops | bytes accessed | tf_op | source)
XLA Modules:
  0.0 96.3 jit_solution(5732335421293734483)
XLA Ops:
  0.0 0.0 copy-start
  0.0 0.8 fusion.8
  0.8 0.1 dynamic_slice.10
  0.9 0.1 broadcast_bitcast_fusion
  1.0 1.7 %broadcast_multiply_fusion.x_ref = bf16[32,4096]{1,0:T(8,128)(2,1)} fusion(bf16[32,4096]{1,0:T(8,128)(2,1)} %param.10, bf16[4096]{0:T(1024)(128)(2,1)S(1)} %bitcast.35), kind=kLoop, calls=%fused_computation.15 | loop fusion | flops 131072 | bytes 532480 | tf_op jit(solution)/shard_map/mul | solution.py:515
  2.7 36.3 %shard_map.100 = (bf16[8,32,4096]{2,1,0:T(8,128)(2,1)}, bf16[8,32,2048]{2,1,0:T(8,128)(2,1)}) custom-call(bf16[32,4096]{1,0:T(8,128)(2,1)} %broadcast_multiply_fusion.x_ref), custom_call_target="tpu_custom_call" | custom-call | tf_op jit(solution)/shard_map/pallas_call | solution.py:236
  39.0 11.9 %convolution_convert_fusion = bf16[256,2048]{1,0:T(8,128)(2,1)} fusion(bf16[256,4096]{1,0:T(8,128)(2,1)} %bitcast.36, bf16[2048,4096]{1,0:T(8,128)(2,1)} %param.12), kind=kOutput, calls=%fused_computation.1 | convolution fusion | flops 4295491584 | bytes 19922944 | tf_op jit(solution)/shard_map/dot_general | solution.py:517
  50.9 0.0 copy-start.5
  50.9 0.0 copy-start.1
  50.9 0.0 copy-start.2
  50.9 22.4 %shard_map.101 = bf16[8,8,2048]{2,1,0:T(8,128)(2,1)} custom-call(bf16[8,2,2,8,2048]{4,3,2,1,0:T(8,128)(2,1)} %bitcast.31), custom_call_target="tpu_custom_call" | custom-call | tf_op jit(solution)/shard_map/pallas_call | solution.py:352
  73.3 1.0 %fusion.9 = (f32[8,8,512]{2,1,0:T(8,128)S(1)}, f32[8,8,512]{2,1,0:T(8,128)S(1)}, f32[8,8,512]{2,1,0:T(8,128)S(1)}, f32[8,8,512]{2,1,0:T(8,128)S(1)}) fusion(bf16[8,8,2048]{2,1,0:T(8,128)(2,1)} %shard_map.101), kind=kLoop, calls=%fused_computation.26 | loop fusion | bytes 1048576 | tf_op jit(solution)/shard_map/slice
  74.3 0.0 copy-start.3
  74.4 0.0 copy-done.5
  74.4 0.1 constant_dynamic-slice_fusion
  74.5 0.0 copy-done.1
  74.5 0.1 copy.20
  74.6 0.0 copy-start.4
  74.6 0.2 multiply_reduce_fusion
  74.8 0.0 copy-done.2
  74.8 0.1 multiply_convert_fusion
  75.0 0.1 copy-done.3
  75.1 0.2 fusion.2
  75.3 0.0 copy-done
  75.3 1.1 %fusion.1.pot_ref = bf16[32,8,512]{2,1,0:T(8,128)(2,1)} fusion(bf16[512,512]{1,0:T(8,128)(2,1)S(1)} %copy-done, f32[32,8,512]{2,1,0:T(8,128)S(1)} %multiply_reduce_fusion, bf16[32,8,512]{2,0,1:T(8,128)(2,1)S(1)} %fusion.2, f32[32]{0:T(128)S(1)} %convert_element_type.50, f32[32,512]{1,0:T(8,128)S(1)} %add.25), kind=kOutput, calls=%fused_computation.5 | convolution fusion | flops 134742016 | bytes 1638528 | tf_op jit(solution)/shard_map/kpc,ac->kpa/dot_general | solution.py:539
  76.4 0.0 copy-done.4
  76.4 0.2 compare_reduce_fusion
  76.6 0.7 broadcast_in_dim.5
  77.3 0.0 copy-start.6
  77.3 16.6 %shard_map.102 = bf16[8,32,256]{2,1,0:T(8,128)(2,1)} custom-call(bf16[32,8,512]{2,1,0:T(8,128)(2,1)} %fusion.1.pot_ref, bf16[4096,1024]{1,0:T(8,128)(2,1)} %lmo_hbm.1, f32[8,1024]{1,0:T(8,128)} %bitcast.34), custom_call_target="tpu_custom_call" | custom-call | tf_op jit(solution)/shard_map/pallas_call | solution.py:464
  93.9 0.0 copy-done.6
  93.9 2.3 %fusion = bf16[256,2048]{1,0:T(8,128)(2,1)} fusion(bf16[8,32,256]{2,1,0:T(8,128)(2,1)} %shard_map.102, bf16[8,32,2048]{2,1,0:T(8,128)(2,1)S(1)} %copy-done.6), kind=kOutput, calls=%fused_computation.2 | convolution fusion | flops 268959744 | bytes 2228224 | tf_op jit(solution)/shard_map/dot_general | solution.py:548
  (6 shorter events, 0.1 us)
Async XLA Ops:
  0.0 75.3 %copy-start = (bf16[512,512]{1,0:T(8,128)(2,1)S(1)}, bf16[512,512]{1,0:T(8,128)(2,1)}, u32[]{:S(2)}) copy-start(bf16[512,512]{1,0:T(8,128)(2,1)} %param.13) | copy-start | bytes 1572868
  50.9 23.5 %copy-start.5 = (f32[3,32]{1,0:T(4,128)S(1)}, f32[3,32]{1,0:T(4,128)}, u32[]{:S(2)}) copy-start(f32[3,32]{1,0:T(4,128)} %param.17) | copy-start | bytes 1156
  50.9 23.6 %copy-start.1 = (f32[3,16384]{1,0:T(4,128)S(1)}, f32[3,16384]{1,0:T(4,128)}, u32[]{:S(2)}) copy-start(f32[3,16384]{1,0:T(4,128)} %param.15) | copy-start | bytes 589828
  50.9 23.9 %copy-start.2 = (f32[16384]{0:T(1024)S(1)}, f32[16384]{0:T(1024)}, u32[]{:S(2)}) copy-start(f32[16384]{0:T(1024)} %param.16) | copy-start | bytes 196612
  74.3 0.7 copy-start.3
  74.6 1.8 %copy-start.4 = (s32[4,16]{1,0:T(4,128)S(1)}, s32[4,16]{1,0:T(4,128)}, u32[]{:S(2)}) copy-start(s32[4,16]{1,0:T(4,128)} %param.19) | copy-start | bytes 772
  77.3 16.7 %copy-start.6 = (bf16[8,32,2048]{2,1,0:T(8,128)(2,1)S(1)}, bf16[8,32,2048]{2,1,0:T(8,128)(2,1)}, u32[]{:S(2)}) copy-start(bf16[8,32,2048]{2,1,0:T(8,128)(2,1)} %get-tuple-element.8) | copy-start | bytes 3145732

commit v3 on v2

--- a/solution.py
+++ b/solution.py
@@ -54,9 +54,44 @@
     return pl.BlockSpec(memory_space=pltpu.VMEM)
 
 
-def spread_kernel(
-    grid_count, tile_count, x_ref, all_ref, rows_ref, zs, zr, ys, yr, es, er, local_sem
+def front_kernel(
+    grid_count,
+    tile_count,
+    x_ref,
+    density_hbm,
+    out_ref,
+    rows_ref,
+    all_ref,
+    density_ref,
+    part_ref,
+    sibling_ref,
+    pair_ref,
+    peer_ref,
+    total_ref,
+    zs,
+    zr,
+    ys,
+    yr,
+    es,
+    er,
+    local_sem,
+    ds,
+    cs,
+    cr,
+    xs,
+    xr,
+    gs,
+    gr,
 ):
+    chunks, slab, width = part_ref.shape[0], part_ref.shape[4], part_ref.shape[5]
+    loads = [
+        pltpu.make_async_copy(
+            density_hbm.at[pl.ds(i * width, width)],
+            density_ref.at[pl.ds(i * width, width)],
+            ds.at[i],
+        )
+        for i in range(chunks)
+    ]
     g, t = lax.axis_index("grid"), lax.axis_index("tile")
     nz, ny = grid_split(grid_count)
     nx, nc = tile_split(tile_count)
@@ -74,7 +109,8 @@
     y_peers = [(z * ny + lax.rem(y + d, ny), t) for d in range(1, ny)]
     x_peers = [(g, lax.rem(x + d, nx) * nc + c) for d in range(1, nx)]
     c_peers = [(g, x * nc + (1 - c))] if nc == 2 else []
-    greet([left, right] + y_peers + x_peers + c_peers)
+    g_peers = [(lax.rem(g + d, grid_count), t) for d in range(1, grid_count)]
+    greet(g_peers + x_peers + c_peers)
 
     def present(k):
         if k == 0:
@@ -155,6 +191,8 @@
     send_block(0)
     keep = pltpu.make_async_copy(x_ref, all_ref.at[g], local_sem)
     keep.start()
+    for load in loads:
+        load.start()
     for step in range(1, nz):
         for k in (2 * step - 1, 2 * step):
 
@@ -175,16 +213,131 @@
     else:
         take_across(0)
     keep.wait()
+    batch = x_ref.shape[0]
+    points = grid_count * batch
+    order = list(range(1, nx)) + [0]
+
+    def product(i):
+        loads[i].wait()
+        value = lax.dot_general(
+            all_ref[...].reshape(points, cols),
+            density_ref[i * width : (i + 1) * width, :],
+            (((1,), (1,)), ((), ())),
+            preferred_element_type=f32,
+        )
+        if slab % 8 == 0:
+            part_ref[i] = value.reshape(grid_count, nx, nc, slab, width).astype(bf16)
+        else:
+            for n in range(points // slab):
+                part_ref[i, n // (nx * nc), n // nc % nx, n % nc] = value[
+                    n * slab : (n + 1) * slab
+                ].astype(bf16)
+
+    def core_copy(i, d):
+        column = lax.rem(x + d, nx)
+        return remote(
+            part_ref.at[i, :, column, 1 - c],
+            sibling_ref.at[i, :, column],
+            cs.at[i, d],
+            cr.at[i, d],
+            c_peers[0],
+        )
+
+    def pair_copy(i, d):
+        return remote(
+            pair_ref.at[i, d], peer_ref.at[i, d], xs.at[i, d], xr.at[i, d], x_peers[d - 1]
+        )
+
+    def exchange(i):
+        for d in order:
+            column = lax.rem(x + d, nx)
+            if nc == 2:
+                core_copy(i, d).wait_recv()
+
+            @pl.loop(0, grid_count)
+            def _(n):
+                value = part_ref[i, n, column, c].astype(f32)
+                if nc == 2:
+                    value = value + sibling_ref[i, n, column].astype(f32)
+                pair_ref[i, d, n] = value.astype(bf16)
+
+            if d:
+                pair_copy(i, d).start()
+
+    def pass_rows():
+        @pl.when(jnp.logical_not(is_owner))
+        def _():
+            for k in steps:
+
+                @pl.when(present(k))
+                def _():
+                    for d in range(ny):
+                        spot = rows_ref.at[source(k, d)]
+                        pass_on = remote(
+                            spot, spot, es.at[nx - 1], er.at[d, k], (c_peers or [right])[0]
+                        )
+                        if nc == 2:
+
+                            @pl.when(in_column)
+                            def _():
+                                pass_on.wait_recv()
+                                pass_on.start()
+
+    own = pltpu.make_async_copy(all_ref.at[:, :, pl.ds(offset, rows)], rows_ref, local_sem)
 
     @pl.when(is_owner)
     def _():
-        own = pltpu.make_async_copy(all_ref.at[:, :, pl.ds(offset, rows)], rows_ref, local_sem)
         own.start()
+
+    for i in range(chunks):
+        product(i)
+        if nc == 2:
+            for d in order:
+                core_copy(i, d).start()
+        if i == 0:
+            pass_rows()
+        else:
+            exchange(i - 1)
+    exchange(chunks - 1)
+
+    for i in range(chunks):
+        for d in range(1, nx):
+            pair_copy(i, d).wait_recv()
+
+        @pl.loop(0, grid_count)
+        def _(n):
+            value = pair_ref[i, 0, n].astype(f32)
+            for d in range(1, nx):
+                value = value + peer_ref[i, d, n].astype(f32)
+            total_ref[n, :, i * width : (i + 1) * width] = value.astype(bf16)
+
+    g_copies = []
+    for d in range(1, grid_count):
+        target = lax.rem(g + d, grid_count)
+        copy = remote(
+            total_ref.at[target], out_ref.at[g], gs.at[d], gr.at[d], g_peers[d - 1]
+        )
+        copy.start()
+        g_copies.append(copy)
+    out_ref[g] = total_ref[g]
+
+    @pl.when(is_owner)
+    def _():
         for i in range(len(x_peers + c_peers)):
             remote(rows_ref, rows_ref, es.at[i], er.at[0, 0], right).wait_send()
         own.wait()
 
-    @pl.when(jnp.logical_not(is_owner))
+    if nc == 2:
+
+        @pl.when(jnp.logical_and(in_column, jnp.logical_not(is_owner)))
+        def _():
+            remote(rows_ref, rows_ref, es.at[nx - 1], er.at[0, 0], right).wait_send()
+
+        waits_rows = jnp.logical_not(in_column)
+    else:
+        waits_rows = jnp.logical_not(is_owner)
+
+    @pl.when(waits_rows)
     def _():
         for k in steps:
 
@@ -192,21 +345,7 @@
             def _():
                 for d in range(ny):
                     spot = rows_ref.at[source(k, d)]
-                    pass_on = remote(
-                        spot, spot, es.at[nx - 1], er.at[d, k], (c_peers or [right])[0]
-                    )
-                    pass_on.wait_recv()
-                    if nc == 2:
-
-                        @pl.when(in_column)
-                        def _():
-                            pass_on.start()
-
-        if nc == 2:
-
-            @pl.when(in_column)
-            def _():
-                remote(rows_ref, rows_ref, es.at[nx - 1], er.at[0, 0], right).wait_send()
+                    remote(spot, spot, es.at[0], er.at[d, k], right).wait_recv()
 
     for k in steps:
 
@@ -227,21 +366,41 @@
             for d in range(1, ny):
                 across(k, d).wait_send()
 
-
-def spread(masked, grid_count, tile_count, rows):
-    points, cols = masked.shape
+    for i in range(chunks):
+        for d in range(nx):
+            if nc == 2:
+                core_copy(i, d).wait_send()
+            if d:
+                pair_copy(i, d).wait_send()
+    for copy in g_copies:
+        copy.wait()
+
+
+def front(masked, density, grid_count, tile_count):
+    batch, cols = masked.shape
+    rows = density.shape[0]
     nz, ny = grid_split(grid_count)
     nx, nc = tile_split(tile_count)
+    slab = batch // tile_count
+    width = min(rows, 512)
+    chunks = rows // width
     dma = pltpu.SemaphoreType.DMA
     return pl.pallas_call(
-        functools.partial(spread_kernel, grid_count, tile_count),
+        functools.partial(front_kernel, grid_count, tile_count),
         out_shape=(
-            jax.ShapeDtypeStruct((grid_count, points, cols), bf16),
-            jax.ShapeDtypeStruct((grid_count, points, rows), bf16),
+            jax.ShapeDtypeStruct((grid_count, slab, rows), bf16),
+            jax.ShapeDtypeStruct((grid_count, batch, rows), bf16),
         ),
-        in_specs=[vmem()],
+        in_specs=[vmem(), pl.BlockSpec(memory_space=pl.ANY)],
         out_specs=(vmem(), vmem()),
         scratch_shapes=[
+            pltpu.VMEM((grid_count, batch, cols), bf16),
+            pltpu.VMEM((rows, cols), bf16),
+            pltpu.VMEM((chunks, grid_count, nx, nc, slab, width), bf16),
+            pltpu.VMEM((chunks, grid_count, nx, slab, width), bf16),
+            pltpu.VMEM((chunks, nx, grid_count, slab, width), bf16),
+            pltpu.VMEM((chunks, nx, grid_count, slab, width), bf16),
+            pltpu.VMEM((grid_count, slab, rows), bf16),
             dma((2, nz)),
             dma((2, nz)),
             dma((ny, 2 * nz)),
@@ -249,125 +408,16 @@
             dma((nx,)),
             dma((ny, 2 * nz)),
             dma,
-        ],
-        compiler_params=params(0),
-    )(masked)
-
-
-def reduce_kernel(
-    grid_count,
-    tile_count,
-    part_ref,
-    out_ref,
-    sibling_ref,
-    pair_ref,
-    peer_ref,
-    total_ref,
-    cs,
-    cr,
-    xs,
-    xr,
-    gs,
-    gr,
-):
-    g, t = lax.axis_index("grid"), lax.axis_index("tile")
-    nx, nc = tile_split(tile_count)
-    x, c = t // nc, t % nc
-    sibling = 1 - c if nc == 2 else c
-    x_peers = [(g, lax.rem(x + d, nx) * nc + c) for d in range(1, nx)]
-    g_peers = [(lax.rem(g + d, grid_count), t) for d in range(1, grid_count)]
-    c_peers = [(g, x * nc + sibling)] if nc == 2 else []
-    greet(c_peers + x_peers + g_peers)
-
-    c_copies = []
-    if nc == 2:
-        for d in range(nx):
-            column = lax.rem(x + d, nx)
-            c_copies.append(
-                remote(
-                    part_ref.at[:, column, sibling],
-                    sibling_ref.at[:, column],
-                    cs.at[d],
-                    cr.at[d],
-                    c_peers[0],
-                )
-            )
-        order = list(range(1, nx)) + [0]
-        for d in order:
-            c_copies[d].start()
-
-    def pair(d):
-        column = lax.rem(x + d, nx)
-        if nc == 2:
-            c_copies[d].wait_recv()
-
-        @pl.loop(0, grid_count)
-        def _(i):
-            value = part_ref[i, column, c].astype(f32)
-            if nc == 2:
-                value = value + sibling_ref[i, column].astype(f32)
-            pair_ref[d, i] = value.astype(bf16)
-
-    x_copies = []
-    for d in range(1, nx):
-        pair(d)
-        copy = remote(
-            pair_ref.at[d], peer_ref.at[d], xs.at[d], xr.at[d], x_peers[d - 1]
-        )
-        copy.start()
-        x_copies.append(copy)
-    pair(0)
-    for copy in x_copies:
-        copy.wait_recv()
-
-    @pl.loop(0, grid_count)
-    def _(i):
-        value = pair_ref[0, i].astype(f32)
-        for d in range(1, nx):
-            value = value + peer_ref[d, i].astype(f32)
-        total_ref[i] = value.astype(bf16)
-
-    g_copies = []
-    for d in range(1, grid_count):
-        target = lax.rem(g + d, grid_count)
-        copy = remote(
-            total_ref.at[target], out_ref.at[g], gs.at[d], gr.at[d], g_peers[d - 1]
-        )
-        copy.start()
-        g_copies.append(copy)
-    out_ref[g] = total_ref[g]
-    for copy in c_copies:
-        copy.wait_send()
-    for copy in x_copies:
-        copy.wait_send()
-    for copy in g_copies:
-        copy.wait()
-
-
-def reduce_parts(parts, grid_count, tile_count):
-    nx, nc = tile_split(tile_count)
-    points, rows = parts.shape
-    slab = points // (grid_count * tile_count)
-    dma = pltpu.SemaphoreType.DMA
-    return pl.pallas_call(
-        functools.partial(reduce_kernel, grid_count, tile_count),
-        out_shape=jax.ShapeDtypeStruct((grid_count, slab, rows), bf16),
-        in_specs=[vmem()],
-        out_specs=vmem(),
-        scratch_shapes=[
-            pltpu.VMEM((grid_count, nx, slab, rows), bf16),
-            pltpu.VMEM((nx, grid_count, slab, rows), bf16),
-            pltpu.VMEM((nx, grid_count, slab, rows), bf16),
-            pltpu.VMEM((grid_count, slab, rows), bf16),
-            dma((nx,)),
-            dma((nx,)),
-            dma((nx,)),
-            dma((nx,)),
+            dma((chunks,)),
+            dma((chunks, nx)),
+            dma((chunks, nx)),
+            dma((chunks, nx)),
+            dma((chunks, nx)),
             dma((grid_count,)),
             dma((grid_count,)),
         ],
-        compiler_params=params(1),
-    )(parts.reshape(grid_count, nx, nc, slab, rows))
+        compiler_params=params(0),
+    )(masked, density)
 
 
 def finish_kernel(
@@ -513,14 +563,7 @@
     named_cols = lax.dynamic_slice_in_dim(named.astype(f32), first_col, col_blocks, 0)
     col_mask = jnp.repeat(named_cols, block_size)
     masked = point_values * col_mask[None, :].astype(bf16)
-    all_values, row_values = spread(masked, grid_count, tile_count, own_rows)
-    parts = lax.dot_general(
-        all_values.reshape(grid_count * points, own_cols),
-        density,
-        (((1,), (1,)), ((), ())),
-        preferred_element_type=f32,
-    ).astype(bf16)
-    summed = reduce_parts(parts, grid_count, tile_count)
+    summed, row_values = front(masked, density, grid_count, tile_count)
     row_blocks = own_rows // block_size
     term = summed.astype(f32).reshape(grid_count, slab, row_blocks, block_size)
     term = jnp.transpose(term, (0, 2, 1, 3)).reshape(all_blocks, slab, block_size)

time: 96.6 us -> 79.3 us (0.82)
  matrix products: 15.5 us -> 3.6 us
  Pallas kernels: 75.4 us -> 70 us
    dot_general x1 -> x0, matrix products: 11.9 us -> none  [shards(): lax.dot_general(all_values.reshape(grid_count * points, own_cols), densit...]
    pallas_call x2 -> x1, Pallas kernels: 58.8 us -> 51.1 us  [front(): pl.pallas_call(functools.partial(front_kernel, grid_count, tile_count), o...]
    pallas_call x1, Pallas kernels: 16.6 us -> 18.9 us  [finish(): pl.pallas_call(functools.partial(finish_kernel, grid_count, tile_count),...]
where the time goes in v3:
time: 79.3 us; the launch traced here: 79.1 us
  Pallas kernels  70 us (88%)
  matrix products  3.6 us (5%)
  other arithmetic  3.09 us (4%)
  local copies, waits for them, and re-layouts  2.22 us (3%)
    pallas_call x1, Pallas kernels, front(): pl.pallas_call(functools.partial(front_kernel, grid_count, tile_count), o...  51.1 us
    pallas_call x1, Pallas kernels, finish(): pl.pallas_call(functools.partial(finish_kernel, grid_count, tile_count),...  18.9 us
    dot_general x1, matrix products, shards(): lax.dot_general(weights.reshape(grid_count * points, weights.shape[2]), r...  2.34 us
    mul x1, other arithmetic, shards(): masked = point_values * col_mask[None, :].astype(bf16)  1.68 us

profile of v3, /device:TPU:0, one launch (start us, length us, event | category | flops | bytes accessed | tf_op | source)
XLA Modules:
  0.0 79.1 jit_solution(16642278508633371843)
XLA Ops:
  0.0 0.0 copy-start
  0.0 0.8 %fusion.8 = pred[32]{0:T(512)(128)(4,1)S(1)} fusion(s32[16]{0:T(128)} %bitcast.31), kind=kLoop, calls=%fused_computation.19 | loop fusion | flops 992 | bytes 96 | tf_op jit(solution)/shard_map/reduce_or | solution.py:561
  0.8 0.1 dynamic_slice.10
  0.9 0.1 broadcast_bitcast_fusion
  1.0 1.7 %broadcast_multiply_fusion.x_ref = bf16[32,4096]{1,0:T(8,128)(2,1)} fusion(bf16[32,4096]{1,0:T(8,128)(2,1)} %param.10, bf16[4096]{0:T(1024)(128)(2,1)S(1)} %bitcast.30), kind=kLoop, calls=%fused_computation.14 | loop fusion | flops 131072 | bytes 532480 | tf_op jit(solution)/shard_map/mul | solution.py:565
  2.7 51.1 %shard_map.100 = (bf16[8,8,2048]{2,1,0:T(8,128)(2,1)}, bf16[8,32,2048]{2,1,0:T(8,128)(2,1)}) custom-call(bf16[32,4096]{1,0:T(8,128)(2,1)} %broadcast_multiply_fusion.x_ref, bf16[2048,4096]{1,0:T(8,128)(2,1)} %density_hbm.1), custom_call_target="tpu_custom_call" | custom-call | tf_op jit(solution)/shard_map/pallas_call | solution.py:388
  53.7 0.0 copy-start.5
  53.7 0.0 copy-start.1
  53.8 0.0 copy-start.2
  53.8 1.0 %fusion.9 = (f32[8,8,512]{2,1,0:T(8,128)S(1)}, f32[8,8,512]{2,1,0:T(8,128)S(1)}, f32[8,8,512]{2,1,0:T(8,128)S(1)}, f32[8,8,512]{2,1,0:T(8,128)S(1)}) fusion(bf16[8,8,2048]{2,1,0:T(8,128)(2,1)} %get-tuple-element.7), kind=kLoop, calls=%fused_computation.25 | loop fusion | bytes 1048576 | tf_op jit(solution)/shard_map/slice
  54.9 0.0 copy-start.3
  54.9 0.0 copy-done.5
  54.9 0.1 constant_dynamic-slice_fusion
  55.0 0.0 copy-done.1
  55.0 0.1 copy.20
  55.0 0.2 multiply_reduce_fusion
  55.3 0.0 copy-done.2
  55.3 0.0 copy-start.4
  55.3 0.1 multiply_convert_fusion
  55.4 0.1 copy-done.3
  55.6 0.2 fusion.2
  55.8 0.0 copy-done
  55.8 1.0 %fusion.1.pot_ref = bf16[32,8,512]{2,1,0:T(8,128)(2,1)} fusion(bf16[512,512]{1,0:T(8,128)(2,1)S(1)} %copy-done, f32[32,8,512]{2,1,0:T(8,128)S(1)} %multiply_reduce_fusion, bf16[32,8,512]{2,0,1:T(8,128)(2,1)S(1)} %fusion.2, f32[32]{0:T(128)S(1)} %convert_element_type.47, f32[32,512]{1,0:T(8,128)S(1)} %add.25), kind=kOutput, calls=%fused_computation.4 | convolution fusion | flops 134742016 | bytes 1638528 | tf_op jit(solution)/shard_map/kpc,ac->kpa/dot_general | solution.py:582
  56.9 0.0 copy-done.4
  56.9 0.2 compare_reduce_fusion
  57.1 0.7 broadcast_in_dim.5
  57.8 0.0 copy-start.6
  57.8 18.9 %shard_map.101 = bf16[8,32,256]{2,1,0:T(8,128)(2,1)} custom-call(bf16[32,8,512]{2,1,0:T(8,128)(2,1)} %fusion.1.pot_ref, bf16[4096,1024]{1,0:T(8,128)(2,1)} %lmo_hbm.1, f32[8,1024]{1,0:T(8,128)} %bitcast.29), custom_call_target="tpu_custom_call" | custom-call | tf_op jit(solution)/shard_map/pallas_call | solution.py:514
  76.7 0.0 copy-done.6
  76.7 2.3 %fusion = bf16[256,2048]{1,0:T(8,128)(2,1)} fusion(bf16[8,32,256]{2,1,0:T(8,128)(2,1)} %shard_map.101, bf16[8,32,2048]{2,1,0:T(8,128)(2,1)S(1)} %copy-done.6), kind=kOutput, calls=%fused_computation.1 | convolution fusion | flops 268959744 | bytes 2228224 | tf_op jit(solution)/shard_map/dot_general | solution.py:591
  (6 shorter events, 0.1 us)
Async XLA Ops:
  0.0 55.8 %copy-start = (bf16[512,512]{1,0:T(8,128)(2,1)S(1)}, bf16[512,512]{1,0:T(8,128)(2,1)}, u32[]{:S(2)}) copy-start(bf16[512,512]{1,0:T(8,128)(2,1)} %param.13) | copy-start | bytes 1572868
  53.7 1.1 %copy-start.5 = (f32[3,32]{1,0:T(4,128)S(1)}, f32[3,32]{1,0:T(4,128)}, u32[]{:S(2)}) copy-start(f32[3,32]{1,0:T(4,128)} %param.17) | copy-start | bytes 1156
  53.7 1.2 %copy-start.1 = (f32[3,16384]{1,0:T(4,128)S(1)}, f32[3,16384]{1,0:T(4,128)}, u32[]{:S(2)}) copy-start(f32[3,16384]{1,0:T(4,128)} %param.15) | copy-start | bytes 589828
  53.8 1.5 %copy-start.2 = (f32[16384]{0:T(1024)S(1)}, f32[16384]{0:T(1024)}, u32[]{:S(2)}) copy-start(f32[16384]{0:T(1024)} %param.16) | copy-start | bytes 196612
  54.9 0.7 copy-start.3
  55.3 1.6 %copy-start.4 = (s32[4,16]{1,0:T(4,128)S(1)}, s32[4,16]{1,0:T(4,128)}, u32[]{:S(2)}) copy-start(s32[4,16]{1,0:T(4,128)} %param.19) | copy-start | bytes 772
  57.8 18.9 %copy-start.6 = (bf16[8,32,2048]{2,1,0:T(8,128)(2,1)S(1)}, bf16[8,32,2048]{2,1,0:T(8,128)(2,1)}, u32[]{:S(2)}) copy-start(bf16[8,32,2048]{2,1,0:T(8,128)(2,1)} %get-tuple-element.8) | copy-start | bytes 3145732

commit v4 on v3

--- a/solution.py
+++ b/solution.py
@@ -54,13 +54,23 @@
     return pl.BlockSpec(memory_space=pltpu.VMEM)
 
 
+def listed(table_ref, row, block_id):
+    flag = jnp.float32(0.0)
+    for i in range(table_ref.shape[1]):
+        flag = jnp.where(table_ref[row, i] == block_id, jnp.float32(1.0), flag)
+    return flag
+
+
 def front_kernel(
+    block_size,
     grid_count,
     tile_count,
-    x_ref,
+    sig_ref,
+    value_ref,
     density_hbm,
     out_ref,
     rows_ref,
+    x_ref,
     all_ref,
     density_ref,
     part_ref,
@@ -110,6 +120,10 @@
     x_peers = [(g, lax.rem(x + d, nx) * nc + c) for d in range(1, nx)]
     c_peers = [(g, x * nc + (1 - c))] if nc == 2 else []
     g_peers = [(lax.rem(g + d, grid_count), t) for d in range(1, grid_count)]
+    for m in range(cols // block_size):
+        lanes = slice(m * block_size, (m + 1) * block_size)
+        flag = listed(sig_ref, 0, t * (cols // block_size) + m)
+        x_ref[:, lanes] = (value_ref[:, lanes].astype(f32) * flag).astype(bf16)
     greet(g_peers + x_peers + c_peers)
 
     def present(k):
@@ -188,6 +202,31 @@
                 def _():
                     share(k, d)
 
+    batch = x_ref.shape[0]
+    halves = 2 if nz % 4 == 0 else 1
+    part_rows = grid_count // halves
+    half = z // (nz // halves)
+
+    def product(i, h):
+        if h == 0:
+            loads[i].wait()
+        group = pl.ds(lax.rem(half + h, halves) * part_rows, part_rows)
+        value = lax.dot_general(
+            all_ref[group].reshape(part_rows * batch, cols),
+            density_ref[i * width : (i + 1) * width, :],
+            (((1,), (1,)), ((), ())),
+            preferred_element_type=f32,
+        )
+        if slab % 8 == 0:
+            part_ref[i, group] = value.reshape(part_rows, nx, nc, slab, width).astype(bf16)
+        else:
+            first = lax.rem(half + h, halves) * part_rows
+            for n in range(part_rows * batch // slab):
+                part_ref[i, first + n // (nx * nc), n // nc % nx, n % nc] = value[
+                    n * slab : (n + 1) * slab
+                ].astype(bf16)
+
+    early = (chunks + 1) // 2
     send_block(0)
     keep = pltpu.make_async_copy(x_ref, all_ref.at[g], local_sem)
     keep.start()
@@ -202,36 +241,26 @@
                 arrived(k, 0, zs.at[lane, step - 1], zr.at[lane, step - 1])
                 send_block(k)
 
+        if halves == 2 and step == nz // 2 + 1:
+            for i in range(early, chunks):
+                product(i, 0)
         if step == 1:
             take_across(0)
         else:
             take_across(2 * step - 3)
             take_across(2 * step - 2)
+        if halves == 2 and step == nz // 2:
+            keep.wait()
+            for i in range(early):
+                product(i, 0)
     if nz > 1:
         take_across(2 * nz - 3)
         take_across(2 * nz - 2)
     else:
         take_across(0)
-    keep.wait()
-    batch = x_ref.shape[0]
-    points = grid_count * batch
+    if halves == 1:
+        keep.wait()
     order = list(range(1, nx)) + [0]
-
-    def product(i):
-        loads[i].wait()
-        value = lax.dot_general(
-            all_ref[...].reshape(points, cols),
-            density_ref[i * width : (i + 1) * width, :],
-            (((1,), (1,)), ((), ())),
-            preferred_element_type=f32,
-        )
-        if slab % 8 == 0:
-            part_ref[i] = value.reshape(grid_count, nx, nc, slab, width).astype(bf16)
-        else:
-            for n in range(points // slab):
-                part_ref[i, n // (nx * nc), n // nc % nx, n % nc] = value[
-                    n * slab : (n + 1) * slab
-                ].astype(bf16)
 
     def core_copy(i, d):
         column = lax.rem(x + d, nx)
@@ -290,7 +319,7 @@
         own.start()
 
     for i in range(chunks):
-        product(i)
+        product(i, halves - 1)
         if nc == 2:
             for d in order:
                 core_copy(i, d).start()
@@ -376,8 +405,12 @@
         copy.wait()
 
 
-def front(masked, density, grid_count, tile_count):
-    batch, cols = masked.shape
+def smem():
+    return pl.BlockSpec(memory_space=pltpu.SMEM)
+
+
+def front(sig_blocks, values, density, block_size, grid_count, tile_count):
+    batch, cols = values.shape
     rows = density.shape[0]
     nz, ny = grid_split(grid_count)
     nx, nc = tile_split(tile_count)
@@ -386,14 +419,15 @@
     chunks = rows // width
     dma = pltpu.SemaphoreType.DMA
     return pl.pallas_call(
-        functools.partial(front_kernel, grid_count, tile_count),
+        functools.partial(front_kernel, block_size, grid_count, tile_count),
         out_shape=(
             jax.ShapeDtypeStruct((grid_count, slab, rows), bf16),
             jax.ShapeDtypeStruct((grid_count, batch, rows), bf16),
         ),
-        in_specs=[vmem(), pl.BlockSpec(memory_space=pl.ANY)],
+        in_specs=[smem(), vmem(), pl.BlockSpec(memory_space=pl.ANY)],
         out_specs=(vmem(), vmem()),
         scratch_shapes=[
+            pltpu.VMEM((batch, cols), bf16),
             pltpu.VMEM((grid_count, batch, cols), bf16),
             pltpu.VMEM((rows, cols), bf16),
             pltpu.VMEM((chunks, grid_count, nx, nc, slab, width), bf16),
@@ -417,7 +451,7 @@
             dma((grid_count,)),
         ],
         compiler_params=params(0),
-    )(masked, density)
+    )(sig_blocks, values, density)
 
 
 def finish_kernel(
@@ -425,7 +459,7 @@
     tile_count,
     pot_ref,
     lmo_hbm,
-    mask_ref,
+    domain_ref,
     all_ref,
     lmo_ref,
     got_ref,
@@ -447,7 +481,8 @@
     t_peers = [(g, lax.rem(t + d, tile_count)) for d in range(1, tile_count)]
     g_peers = [(lax.rem(g + d, grid_count), t) for d in range(1, grid_count)]
     greet(t_peers + g_peers)
-    cols = mask_ref.shape[0]
+    cols = got_ref.shape[1]
+    strips = domain_ref.shape[0]
     slab = pot_ref.shape[1]
     block = pot_ref.shape[2]
     strip = own_ref.shape[1]
@@ -465,23 +500,27 @@
         copy.start()
         v_copies.append(copy)
     got_ref[t] = pot_ref[pl.ds(t * cols, cols)]
+    flags = [[listed(domain_ref, s, t * cols + m) for m in range(cols)] for s in range(strips)]
     for copy in v_copies:
         copy.wait()
     for i in range(tile_count):
         for m in range(cols):
             flat_ref[m, i * slab : (i + 1) * slab, :] = got_ref[i, m].astype(f32)
     load.wait()
-    for s in range(tile_count):
-        lanes = slice(s * strip, (s + 1) * strip)
+    width = lmo_ref.shape[1] // strips
+    per_tile = strips // tile_count
+    for s in range(strips):
+        lanes = slice(s * width, (s + 1) * width)
         total = None
         for m in range(cols):
-            term = mask_ref[m : m + 1, lanes] * jnp.dot(
+            term = flags[s][m] * jnp.dot(
                 flat_ref[m].astype(bf16),
                 lmo_ref[m * block : (m + 1) * block, lanes],
                 preferred_element_type=f32,
             )
             total = term if total is None else total + term
-        send_ref[s] = total.astype(bf16)
+        first = s % per_tile * width
+        send_ref[s // per_tile, :, first : first + width] = total.astype(bf16)
     w_copies = []
     for d in range(1, tile_count):
         target = lax.rem(t + d, tile_count)
@@ -505,7 +544,7 @@
         copy.wait()
 
 
-def finish(potential, lmo_coeffs, mask, batch, grid_count, tile_count):
+def finish(potential, lmo_coeffs, domain_blocks, batch, grid_count, tile_count):
     blocks, slab, block = potential.shape
     cols = blocks // tile_count
     total = lmo_coeffs.shape[1]
@@ -514,7 +553,7 @@
     return pl.pallas_call(
         functools.partial(finish_kernel, grid_count, tile_count),
         out_shape=jax.ShapeDtypeStruct((grid_count, batch, strip), bf16),
-        in_specs=[vmem(), pl.BlockSpec(memory_space=pl.ANY), vmem()],
+        in_specs=[vmem(), pl.BlockSpec(memory_space=pl.ANY), smem()],
         out_specs=vmem(),
         scratch_shapes=[
             pltpu.VMEM(lmo_coeffs.shape, bf16),
@@ -532,7 +571,7 @@
             dma((grid_count,)),
         ],
         compiler_params=params(2),
-    )(potential, lmo_coeffs, mask)
+    )(potential, lmo_coeffs, domain_blocks)
 
 
 def shards(
@@ -555,15 +594,12 @@
     block_size = coulomb_core.shape[0]
     total_aos = ao_widths.shape[0]
     all_blocks = total_aos // block_size
-    col_blocks = own_cols // block_size
     slab = points // tile_count
     block_ids = jnp.arange(all_blocks, dtype=jnp.int32)
     named = jnp.any(sig_blocks[0][:, None] == block_ids[None, :], axis=0)
-    first_col = panel * col_blocks
-    named_cols = lax.dynamic_slice_in_dim(named.astype(f32), first_col, col_blocks, 0)
-    col_mask = jnp.repeat(named_cols, block_size)
-    masked = point_values * col_mask[None, :].astype(bf16)
-    summed, row_values = front(masked, density, grid_count, tile_count)
+    summed, row_values = front(
+        sig_blocks, point_values, density, block_size, grid_count, tile_count
+    )
     row_blocks = own_rows // block_size
     term = summed.astype(f32).reshape(grid_count, slab, row_blocks, block_size)
     term = jnp.transpose(term, (0, 2, 1, 3)).reshape(all_blocks, slab, block_size)
@@ -583,11 +619,7 @@
         "kpc,ac->kpa", screened, coulomb_core, preferred_element_type=f32
     )
     potential = (scaled * mixed).astype(bf16)
-    local_ids = first_col + jnp.arange(col_blocks, dtype=jnp.int32)
-    in_domain = jnp.any(domain_blocks[:, :, None] == local_ids[None, None, :], axis=1)
-    strip_width = lmo_coeffs.shape[1] // domain_blocks.shape[0]
-    mask = jnp.repeat(jnp.transpose(in_domain).astype(f32), strip_width, axis=1)
-    weights = finish(potential, lmo_coeffs, mask, points, grid_count, tile_count)
+    weights = finish(potential, lmo_coeffs, domain_blocks, points, grid_count, tile_count)
     return lax.dot_general(
         weights.reshape(grid_count * points, weights.shape[2]),
         row_values.reshape(grid_count * points, own_rows),

time: 79.3 us -> 77.8 us (0.981)
  other arithmetic: 3.09 us -> 0.49 us
  Pallas kernels: 70 us -> 72.1 us
  local copies, waits for them, and re-layouts: 2.22 us -> 1.27 us
    mul x1 -> x0, other arithmetic: 1.68 us -> none  [shards(): masked = point_values * col_mask[None, :].astype(bf16)]
    pallas_call x1, Pallas kernels: 51.1 us -> 52.5 us  [front(): pl.pallas_call(functools.partial(front_kernel, block_size, grid_count, ti...]
where the time goes in v4:
time: 77.8 us; the launch traced here: 77.6 us
  Pallas kernels  72.1 us (93%)
  matrix products  3.6 us (5%)
  local copies, waits for them, and re-layouts  1.27 us (2%)
    pallas_call x1, Pallas kernels, front(): pl.pallas_call(functools.partial(front_kernel, block_size, grid_count, ti...  52.5 us
    pallas_call x1, Pallas kernels, finish(): pl.pallas_call(functools.partial(finish_kernel, grid_count, tile_count),...  19.6 us
    dot_general x1, matrix products, shards(): lax.dot_general(weights.reshape(grid_count * points, weights.shape[2]), r...  2.33 us

profile of v4, /device:TPU:0, one launch (start us, length us, event | category | flops | bytes accessed | tf_op | source)
XLA Modules:
  0.0 77.6 jit_solution(8025792648732151535)
XLA Ops:
  0.0 0.0 copy-start
  0.0 52.5 %shard_map.100 = (bf16[8,8,2048]{2,1,0:T(8,128)(2,1)}, bf16[8,32,2048]{2,1,0:T(8,128)(2,1)}) custom-call(s32[1,16]{1,0:T(1,128)} %sig_ref.1, bf16[32,4096]{1,0:T(8,128)(2,1)} %value_ref.1, bf16[2048,4096]{1,0:T(8,128)(2,1)} %density_hbm.1), custom_call_target="tpu_custom_call" | custom-call | tf_op jit(solution)/shard_map/pallas_call | solution.py:421
  52.5 0.0 copy-start.4
  52.5 0.0 copy-start.1
  52.5 0.0 copy-start.2
  52.6 0.0 copy-start.5
  52.6 1.0 %fusion.9 = (f32[8,8,512]{2,1,0:T(8,128)S(1)}, f32[8,8,512]{2,1,0:T(8,128)S(1)}, f32[8,8,512]{2,1,0:T(8,128)S(1)}, f32[8,8,512]{2,1,0:T(8,128)S(1)}) fusion(bf16[8,8,2048]{2,1,0:T(8,128)(2,1)} %get-tuple-element.7), kind=kLoop, calls=%fused_computation.19 | loop fusion | bytes 1048576 | tf_op jit(solution)/shard_map/slice
  53.7 0.0 copy-start.3
  53.7 0.0 copy-done.4
  53.7 0.1 constant_dynamic-slice_fusion
  53.8 0.0 copy-done.1
  53.8 0.1 copy.19
  53.8 0.2 multiply_reduce_fusion
  54.1 0.0 copy-done.2
  54.1 0.0 copy-done.5
  54.1 0.1 fusion.8
  54.2 0.1 multiply_convert_fusion
  54.3 0.1 copy-done.3
  54.4 0.2 fusion.2
  54.6 0.0 copy-done
  54.6 1.0 %fusion.1.pot_ref = bf16[32,8,512]{2,1,0:T(8,128)(2,1)} fusion(bf16[512,512]{1,0:T(8,128)(2,1)S(1)} %copy-done, f32[32,8,512]{2,1,0:T(8,128)S(1)} %multiply_reduce_fusion, bf16[32,8,512]{2,0,1:T(8,128)(2,1)S(1)} %fusion.2, f32[32]{0:T(128)S(1)} %convert_element_type.28, f32[32,512]{1,0:T(8,128)S(1)} %add.14), kind=kOutput, calls=%fused_computation.4 | convolution fusion | flops 134742016 | bytes 1638528 | tf_op jit(solution)/shard_map/kpc,ac->kpa/dot_general | solution.py:618
  55.7 0.0 copy-start.6
  55.7 19.6 %shard_map.101 = bf16[8,32,256]{2,1,0:T(8,128)(2,1)} custom-call(bf16[32,8,512]{2,1,0:T(8,128)(2,1)} %fusion.1.pot_ref, bf16[4096,1024]{1,0:T(8,128)(2,1)} %lmo_hbm.1, s32[4,16]{1,0:T(4,128)} %domain_ref.1), custom_call_target="tpu_custom_call" | custom-call | tf_op jit(solution)/shard_map/pallas_call | solution.py:553
  75.3 0.0 copy-done.6
  75.3 2.3 %fusion = bf16[256,2048]{1,0:T(8,128)(2,1)} fusion(bf16[8,32,256]{2,1,0:T(8,128)(2,1)} %shard_map.101, bf16[8,32,2048]{2,1,0:T(8,128)(2,1)S(1)} %copy-done.6), kind=kOutput, calls=%fused_computation.1 | convolution fusion | flops 268959744 | bytes 2228224 | tf_op jit(solution)/shard_map/dot_general | solution.py:623
  (3 shorter events, 0.1 us)
Async XLA Ops:
  0.0 54.6 %copy-start = (bf16[512,512]{1,0:T(8,128)(2,1)S(1)}, bf16[512,512]{1,0:T(8,128)(2,1)}, u32[]{:S(2)}) copy-start(bf16[512,512]{1,0:T(8,128)(2,1)} %param.13) | copy-start | bytes 1572868
  52.5 1.2 %copy-start.4 = (f32[3,32]{1,0:T(4,128)S(1)}, f32[3,32]{1,0:T(4,128)}, u32[]{:S(2)}) copy-start(f32[3,32]{1,0:T(4,128)} %param.17) | copy-start | bytes 1156
  52.5 1.2 %copy-start.1 = (f32[3,16384]{1,0:T(4,128)S(1)}, f32[3,16384]{1,0:T(4,128)}, u32[]{:S(2)}) copy-start(f32[3,16384]{1,0:T(4,128)} %param.15) | copy-start | bytes 589828
  52.5 1.5 %copy-start.2 = (f32[16384]{0:T(1024)S(1)}, f32[16384]{0:T(1024)}, u32[]{:S(2)}) copy-start(f32[16384]{0:T(1024)} %param.16) | copy-start | bytes 196612
  52.6 1.5 %copy-start.5 = (s32[1,16]{1,0:T(1,128)S(1)}, s32[1,16]{1,0:T(1,128)}, u32[]{:S(2)}) copy-start(s32[1,16]{1,0:T(1,128)} %sig_ref.1) | copy-start | bytes 196
  53.7 0.7 copy-start.3
  55.7 19.6 %copy-start.6 = (bf16[8,32,2048]{2,1,0:T(8,128)(2,1)S(1)}, bf16[8,32,2048]{2,1,0:T(8,128)(2,1)}, u32[]{:S(2)}) copy-start(bf16[8,32,2048]{2,1,0:T(8,128)(2,1)} %get-tuple-element.8) | copy-start | bytes 3145732

commit v5 on v4

--- a/solution.py
+++ b/solution.py
@@ -37,10 +37,12 @@
     )
 
 
-def greet(devices):
+def greet(devices, work=None):
     barrier = pltpu.get_barrier_semaphore()
     for device in devices:
         pl.semaphore_signal(barrier, inc=1, device_id=device, device_id_type=MESH)
+    if work is not None:
+        work()
     pl.semaphore_wait(barrier, len(devices))
 
 
@@ -120,11 +122,14 @@
     x_peers = [(g, lax.rem(x + d, nx) * nc + c) for d in range(1, nx)]
     c_peers = [(g, x * nc + (1 - c))] if nc == 2 else []
     g_peers = [(lax.rem(g + d, grid_count), t) for d in range(1, grid_count)]
-    for m in range(cols // block_size):
-        lanes = slice(m * block_size, (m + 1) * block_size)
-        flag = listed(sig_ref, 0, t * (cols // block_size) + m)
-        x_ref[:, lanes] = (value_ref[:, lanes].astype(f32) * flag).astype(bf16)
-    greet(g_peers + x_peers + c_peers)
+
+    def make_mask():
+        for m in range(cols // block_size):
+            lanes = slice(m * block_size, (m + 1) * block_size)
+            flag = listed(sig_ref, 0, t * (cols // block_size) + m)
+            x_ref[:, lanes] = (value_ref[:, lanes].astype(f32) * flag).astype(bf16)
+
+    greet(g_peers + x_peers + c_peers, make_mask)
 
     def present(k):
         if k == 0:
@@ -203,30 +208,23 @@
                     share(k, d)
 
     batch = x_ref.shape[0]
-    halves = 2 if nz % 4 == 0 else 1
-    part_rows = grid_count // halves
-    half = z // (nz // halves)
-
-    def product(i, h):
-        if h == 0:
-            loads[i].wait()
-        group = pl.ds(lax.rem(half + h, halves) * part_rows, part_rows)
+
+    def product(i):
+        loads[i].wait()
         value = lax.dot_general(
-            all_ref[group].reshape(part_rows * batch, cols),
+            all_ref[...].reshape(grid_count * batch, cols),
             density_ref[i * width : (i + 1) * width, :],
             (((1,), (1,)), ((), ())),
             preferred_element_type=f32,
         )
         if slab % 8 == 0:
-            part_ref[i, group] = value.reshape(part_rows, nx, nc, slab, width).astype(bf16)
+            part_ref[i] = value.reshape(grid_count, nx, nc, slab, width).astype(bf16)
         else:
-            first = lax.rem(half + h, halves) * part_rows
-            for n in range(part_rows * batch // slab):
-                part_ref[i, first + n // (nx * nc), n // nc % nx, n % nc] = value[
+            for n in range(grid_count * batch // slab):
+                part_ref[i, n // (nx * nc), n // nc % nx, n % nc] = value[
                     n * slab : (n + 1) * slab
                 ].astype(bf16)
 
-    early = (chunks + 1) // 2
     send_block(0)
     keep = pltpu.make_async_copy(x_ref, all_ref.at[g], local_sem)
     keep.start()
@@ -241,25 +239,17 @@
                 arrived(k, 0, zs.at[lane, step - 1], zr.at[lane, step - 1])
                 send_block(k)
 
-        if halves == 2 and step == nz // 2 + 1:
-            for i in range(early, chunks):
-                product(i, 0)
         if step == 1:
             take_across(0)
         else:
             take_across(2 * step - 3)
             take_across(2 * step - 2)
-        if halves == 2 and step == nz // 2:
-            keep.wait()
-            for i in range(early):
-                product(i, 0)
     if nz > 1:
         take_across(2 * nz - 3)
         take_across(2 * nz - 2)
     else:
         take_across(0)
-    if halves == 1:
-        keep.wait()
+    keep.wait()
     order = list(range(1, nx)) + [0]
 
     def core_copy(i, d):
@@ -319,7 +309,7 @@
         own.start()
 
     for i in range(chunks):
-        product(i, halves - 1)
+        product(i)
         if nc == 2:
             for d in order:
                 core_copy(i, d).start()

time: 77.8 us -> 75.9 us (0.976)
  Pallas kernels: 72.1 us -> 70.1 us
    pallas_call x1, Pallas kernels: 52.5 us -> 51.2 us  [front(): pl.pallas_call(functools.partial(front_kernel, block_size, grid_count, ti...]
where the time goes in v5:
time: 75.9 us; the launch traced here: 75.7 us
  Pallas kernels  70.1 us (92%)
  matrix products  3.61 us (5%)
  local copies, waits for them, and re-layouts  1.27 us (2%)
    pallas_call x1, Pallas kernels, front(): pl.pallas_call(functools.partial(front_kernel, block_size, grid_count, ti...  51.2 us
    pallas_call x1, Pallas kernels, finish(): pl.pallas_call(functools.partial(finish_kernel, grid_count, tile_count),...  19 us
    dot_general x1, matrix products, shards(): lax.dot_general(weights.reshape(grid_count * points, weights.shape[2]), r...  2.34 us

profile of v5, /device:TPU:0, one launch (start us, length us, event | category | flops | bytes accessed | tf_op | source)
XLA Modules:
  0.0 75.7 jit_solution(2229496818821122926)
XLA Ops:
  0.0 0.0 copy-start
  0.0 51.2 %shard_map.100 = (bf16[8,8,2048]{2,1,0:T(8,128)(2,1)}, bf16[8,32,2048]{2,1,0:T(8,128)(2,1)}) custom-call(s32[1,16]{1,0:T(1,128)} %sig_ref.1, bf16[32,4096]{1,0:T(8,128)(2,1)} %value_ref.1, bf16[2048,4096]{1,0:T(8,128)(2,1)} %density_hbm.1), custom_call_target="tpu_custom_call" | custom-call | tf_op jit(solution)/shard_map/pallas_call | solution.py:411
  51.2 0.0 copy-start.4
  51.2 0.0 copy-start.1
  51.2 0.0 copy-start.2
  51.2 0.0 copy-start.5
  51.2 1.0 %fusion.9 = (f32[8,8,512]{2,1,0:T(8,128)S(1)}, f32[8,8,512]{2,1,0:T(8,128)S(1)}, f32[8,8,512]{2,1,0:T(8,128)S(1)}, f32[8,8,512]{2,1,0:T(8,128)S(1)}) fusion(bf16[8,8,2048]{2,1,0:T(8,128)(2,1)} %get-tuple-element.7), kind=kLoop, calls=%fused_computation.19 | loop fusion | bytes 1048576 | tf_op jit(solution)/shard_map/slice
  52.3 0.0 copy-start.3
  52.3 0.0 copy-done.4
  52.3 0.1 constant_dynamic-slice_fusion
  52.4 0.0 copy-done.1
  52.4 0.1 copy.19
  52.5 0.2 multiply_reduce_fusion
  52.7 0.0 copy-done.2
  52.8 0.0 copy-done.5
  52.8 0.1 fusion.8
  52.9 0.1 multiply_convert_fusion
  53.0 0.1 copy-done.3
  53.0 0.2 fusion.2
  53.3 0.0 copy-done
  53.3 1.0 %fusion.1.pot_ref = bf16[32,8,512]{2,1,0:T(8,128)(2,1)} fusion(bf16[512,512]{1,0:T(8,128)(2,1)S(1)} %copy-done, f32[32,8,512]{2,1,0:T(8,128)S(1)} %multiply_reduce_fusion, bf16[32,8,512]{2,0,1:T(8,128)(2,1)S(1)} %fusion.2, f32[32]{0:T(128)S(1)} %convert_element_type.28, f32[32,512]{1,0:T(8,128)S(1)} %add.14), kind=kOutput, calls=%fused_computation.4 | convolution fusion | flops 134742016 | bytes 1638528 | tf_op jit(solution)/shard_map/kpc,ac->kpa/dot_general | solution.py:608
  54.3 0.0 copy-start.6
  54.3 19.0 %shard_map.101 = bf16[8,32,256]{2,1,0:T(8,128)(2,1)} custom-call(bf16[32,8,512]{2,1,0:T(8,128)(2,1)} %fusion.1.pot_ref, bf16[4096,1024]{1,0:T(8,128)(2,1)} %lmo_hbm.1, s32[4,16]{1,0:T(4,128)} %domain_ref.1), custom_call_target="tpu_custom_call" | custom-call | tf_op jit(solution)/shard_map/pallas_call | solution.py:543
  73.3 0.0 copy-done.6
  73.3 2.3 %fusion = bf16[256,2048]{1,0:T(8,128)(2,1)} fusion(bf16[8,32,256]{2,1,0:T(8,128)(2,1)} %shard_map.101, bf16[8,32,2048]{2,1,0:T(8,128)(2,1)S(1)} %copy-done.6), kind=kOutput, calls=%fused_computation.1 | convolution fusion | flops 268959744 | bytes 2228224 | tf_op jit(solution)/shard_map/dot_general | solution.py:613
  (3 shorter events, 0.1 us)
Async XLA Ops:
  0.0 53.3 %copy-start = (bf16[512,512]{1,0:T(8,128)(2,1)S(1)}, bf16[512,512]{1,0:T(8,128)(2,1)}, u32[]{:S(2)}) copy-start(bf16[512,512]{1,0:T(8,128)(2,1)} %param.13) | copy-start | bytes 1572868
  51.2 1.2 %copy-start.4 = (f32[3,32]{1,0:T(4,128)S(1)}, f32[3,32]{1,0:T(4,128)}, u32[]{:S(2)}) copy-start(f32[3,32]{1,0:T(4,128)} %param.17) | copy-start | bytes 1156
  51.2 1.2 %copy-start.1 = (f32[3,16384]{1,0:T(4,128)S(1)}, f32[3,16384]{1,0:T(4,128)}, u32[]{:S(2)}) copy-start(f32[3,16384]{1,0:T(4,128)} %param.15) | copy-start | bytes 589828
  51.2 1.5 %copy-start.2 = (f32[16384]{0:T(1024)S(1)}, f32[16384]{0:T(1024)}, u32[]{:S(2)}) copy-start(f32[16384]{0:T(1024)} %param.16) | copy-start | bytes 196612
  51.2 1.5 %copy-start.5 = (s32[1,16]{1,0:T(1,128)S(1)}, s32[1,16]{1,0:T(1,128)}, u32[]{:S(2)}) copy-start(s32[1,16]{1,0:T(1,128)} %sig_ref.1) | copy-start | bytes 196
  52.3 0.7 copy-start.3
  54.3 19.0 %copy-start.6 = (bf16[8,32,2048]{2,1,0:T(8,128)(2,1)S(1)}, bf16[8,32,2048]{2,1,0:T(8,128)(2,1)}, u32[]{:S(2)}) copy-start(bf16[8,32,2048]{2,1,0:T(8,128)(2,1)} %get-tuple-element.8) | copy-start | bytes 3145732
